TPU v7x, 512 devices: a whole 4x4x16 slice. The times are simulated.
512 devices in a mesh: wave: 64 (over z, x), lev: 8 (over y, core).
Axes of the slice: x: 4, y: 4, z: 16, core: 2. Of those that a mesh axis runs over, the one named last changes fastest.
Arguments:
- spectral: bfloat16 [64, 640, 2, 1024], P('wave', None, None, 'lev'), may hold values from -6 to 6
- legendre: bfloat16 [64, 1280, 640], P('wave'), may hold values from -0.25 to 0.25
- pattern: int32 [64, 10, 5], replicated, may hold values from 0 to 1, as said below
- assignment: int32 [64], replicated, may hold values from 0 to 63, each once
- quad_weight: float32 [1280], replicated, may hold values from 0.25 to 2
- coupling: bfloat16 [128, 128], replicated, may hold values from -1 to 2
Outputs:
- tendency: bfloat16 [64, 640, 2, 1024], P('wave', None, None, 'lev')
Inputs may be any that keep to these rules, and one draw needn't show every extreme that they name: For each wavenumber m and degree block k, the latitude blocks with pattern 1 form a band symmetric about the equator that holds the two middle blocks; wavenumber 0 keeps all blocks.
All inputs are finite; a program needn't handle non-finite values.
Results may differ from a plain program's by a relative error of at most 0.0095.
Values may be sent and summed in bfloat16 or wider, within the bound.
No kernel may reach another device: no remote copies, remote signals or barrier semaphores. Data moves between devices by JAX's collectives and lax.ppermute only.
A program may use at most 64 MiB of HBM per device.

v0:
```python
import math

import jax
import jax.numpy as jnp
from jax import lax
from jax.sharding import PartitionSpec as P

F = 8
TILE = 128


def expand_tiles(selected):
    return jnp.repeat(jnp.repeat(selected, TILE, axis=1), TILE, axis=2)


def dft_tables(wavenums, lon_count):
    wave_total = wavenums.shape[0]
    longitudes = jnp.arange(lon_count, dtype=jnp.int32)
    phases = longitudes[:, None] * wavenums[None, :] % lon_count
    angles = phases.astype(jnp.float32) * (2.0 * math.pi / lon_count)
    cosines = jnp.cos(angles)
    sines = jnp.sin(angles)
    synthesis = jnp.stack([cosines, -sines], axis=2).reshape(lon_count, 2 * wave_total) / math.sqrt(
        wave_total
    )
    analysis = jnp.stack([cosines.T, -sines.T], axis=1).reshape(
        2 * wave_total, lon_count
    ) / math.sqrt(lon_count)
    return (synthesis.astype(jnp.bfloat16), analysis.astype(jnp.bfloat16))


def nonlinear(latitude_coeffs, synthesis, analysis, wave_total, channels):
    coeffs = latitude_coeffs.reshape(2 * wave_total, channels)
    field = jnp.dot(synthesis, coeffs, preferred_element_type=jnp.float32)
    shaped = field.reshape(field.shape[0], channels // F, F)
    product = (
        (shaped * jnp.roll(shaped, -1, axis=2))
        .astype(jnp.bfloat16)
        .reshape(field.shape[0], channels)
    )
    returned = jnp.dot(analysis, product, preferred_element_type=jnp.float32)
    return returned.astype(jnp.bfloat16).reshape(wave_total, 2, channels)


def local(spectral, legendre, pattern, assignment, quad_weight, coupling):
    slot_count = spectral.shape[0]
    degrees = spectral.shape[1]
    channels = spectral.shape[3]
    lat_count = legendre.shape[1]
    wave_total = assignment.shape[0]
    first_slot = lax.axis_index("wave") * slot_count
    own_waves = lax.dynamic_slice_in_dim(assignment, first_slot, slot_count)
    picker = (own_waves[:, None] == jnp.arange(wave_total, dtype=jnp.int32)[None, :]).astype(
        jnp.float32
    )
    own_mask = jnp.einsum("sm,mtk->stk", picker, pattern.astype(jnp.float32))
    flattened = spectral.reshape(slot_count, degrees, 2 * channels)
    pruned = legendre * expand_tiles(own_mask).astype(jnp.bfloat16)
    at_lats = jnp.einsum("sln,snc->slc", pruned, flattened, preferred_element_type=jnp.float32)
    at_lats = at_lats.astype(jnp.bfloat16).reshape(slot_count, lat_count, 2, channels)
    by_latitude = lax.all_to_all(at_lats, "wave", split_axis=1, concat_axis=0, tiled=True)
    synthesis, analysis = dft_tables(assignment, 3 * wave_total)
    lat_local = by_latitude.shape[1]

    def per_latitude(lat_index):
        column = lax.dynamic_index_in_dim(by_latitude, lat_index, 1, keepdims=False)
        return nonlinear(column, synthesis, analysis, wave_total, channels)

    returned = lax.map(per_latitude, jnp.arange(lat_local, dtype=jnp.int32))
    by_wave = lax.all_to_all(returned, "wave", split_axis=1, concat_axis=0, tiled=True)
    weighted = (quad_weight[:, None, None, None] * by_wave.astype(jnp.float32)).astype(jnp.bfloat16)
    weighted = weighted.reshape(lat_count, slot_count, 2 * channels)
    spectral_new = jnp.einsum("sln,lsc->snc", pruned, weighted, preferred_element_type=jnp.float32)
    spectral_new = spectral_new.astype(jnp.bfloat16).reshape(slot_count, degrees, 2, channels)
    own_level_count = channels // F
    level_total = coupling.shape[0]
    own_first = lax.axis_index("lev") * own_level_count
    columns = lax.dynamic_slice_in_dim(coupling, own_first, own_level_count, 1)
    levels = spectral_new.reshape(slot_count, degrees, 2, own_level_count, F)
    term = jnp.einsum("ab,sncbf->sncaf", columns, levels, preferred_element_type=jnp.float32)
    term = term.reshape(slot_count, degrees, 2, level_total * F)
    return lax.psum_scatter(term.astype(jnp.bfloat16), "lev", scatter_dimension=3, tiled=True)


def solution(mesh):
    placed = (P("wave", None, None, "lev"), P("wave", None, None), P(), P(), P(), P())
    return jax.shard_map(
        local, mesh=mesh, in_specs=placed, out_specs=P("wave", None, None, "lev"), check_vma=False
    )
```

profile of v0, /device:TPU:6, one launch (start us, length us, event | category | flops | bytes accessed | tf_op | source)
XLA Modules:
  0.0 241.8 jit_solution(14910461114142401641)
XLA Ops:
  6.5 1.2 dynamic_slice.14
  7.8 1.6 fusion.27
  9.6 2.7 %copy.33 = bf16[1,1280,640]{1,2,0:T(8,128)(2,1)S(1)} copy(bf16[1,1280,640]{2,1,0:T(8,128)(2,1)} %param.9) | data formatting | bytes 3276800 | tf_op args[1]
  12.5 0.8 copy-done.3
  13.3 0.7 convolution_convert_fusion.1
  14.1 1.8 copy.34
  15.9 18.6 %all-to-all-start = ((bf16[1,1280,2,128]{3,2,0,1:T(2,128)(2,1)}), bf16[1,1280,2,128]{3,2,0,1:T(2,128)(2,1)S(1)}, u32[]{:S(2)}, u32[]{:S(2)}) async-start(bf16[1,1280,2,128]{3,2,0,1:T(2,128)(2,1)} %copy.34), calls=%async_computation | async-start | bytes 1310720 | tf_op jit(solution)/shard_map/all_to_all | solution.py:61
  35.6 37.2 %all-to-all-done = bf16[1,1280,2,128]{3,2,0,1:T(2,128)(2,1)S(1)} async-done(((bf16[1,1280,2,128]{3,2,0,1:T(2,128)(2,1)}), bf16[1,1280,2,128]{3,2,0,1:T(2,128)(2,1)S(1)}, u32[]{:S(2)}, u32[]{:S(2)}) %all-to-all-start) | async-done | bytes 655392 | tf_op jit(solution)/shard_map/all_to_all | solution.py:61
  72.8 75.9 %while.10 = (s32[]{:T(128)}, bf16[20,64,2,128]{3,2,0,1:T(2,128)(2,1)}, s32[20]{0:T(128)S(1)}, bf16[64,20,2,128]{3,2,1,0:T(2,128)(2,1)S(1)}, bf16[192,128]{1,0:T(...) while((s32[]{:T(128)}, bf16[20,64,2,128]{3,2,0,1:T(2,128)(2,1)}, ...), condition=%wide.region_1.2_spmd, body=%wide.region_0.1_spmd.sunk | while | flops 12673029 | bytes 1376411 | solution.py:69
  75.9 0.7 constant_dynamic-update-slice_fusion.2
  87.3 0.7 constant_dynamic-update-slice_fusion.2
  91.1 0.7 constant_dynamic-update-slice_fusion.2
  94.9 0.7 constant_dynamic-update-slice_fusion.2
  98.7 0.7 constant_dynamic-update-slice_fusion.2
  125.3 0.7 constant_dynamic-update-slice_fusion.2
  132.8 0.7 constant_dynamic-update-slice_fusion.2
  148.7 5.9 %all-to-all-start.1 = ((bf16[20,64,2,128]{3,2,0,1:T(2,128)(2,1)}), bf16[20,64,2,128]{3,2,0,1:T(2,128)(2,1)S(1)}, u32[]{:S(2)}, u32[]{:S(2)}) async-start(bf16[20,64,2,128]{3,2,0,1:T(2,128)(2,1)} %get-tuple-element.37), calls=%async_computation.1 | async-start | bytes 1310720 | tf_op jit(solution)/shard_map/all_to_all | solution.py:70
  154.7 37.4 %all-to-all-done.1 = bf16[20,64,2,128]{3,2,0,1:T(2,128)(2,1)S(1)} async-done(((bf16[20,64,2,128]{3,2,0,1:T(2,128)(2,1)}), bf16[20,64,2,128]{3,2,0,1:T(2,128)(2,1)S(1)}, u32[]{:S(2)}, u32[]{:S(2)}) %all-to-all-start.1) | async-done | bytes 655392 | tf_op jit(solution)/shard_map/all_to_all | solution.py:70
  192.1 1.6 fusion.4
  193.8 0.8 fusion.5
  194.5 0.9 convert_bitcast_fusion
  195.4 3.0 %copy.63 = bf16[1,640,2,128,8]{1,4,3,2,0:T(8,128)(2,1)} copy(bf16[1,640,2,128,8]{1,3,4,2,0:T(8,128)(2,1)S(1)} %convert_bitcast_fusion) | data formatting | bytes 5242880 | tf_op jit(solution)/shard_map/convert_element_type | solution.py:82
  198.5 34.5 %reduce-scatter.2.cloned.1.call-done = bf16[1,640,2,128]{1,3,2,0:T(8,128)(2,1)} async-done(((bf16[1,640,2,1024]{1,3,2,0:T(8,128)(2,1)}), bf16[1,640,2,128]{1,3,2,0:T(8,128)(2,1)}) %reduce-scatter.2.cloned.1.call-update) | async-done | bytes 327696 | tf_op jit(solution)/shard_map/reduce_scatter | solution.py:82
  233.0 1.9 copy.42
  (218 shorter events, 33.5 us)
Async XLA Ops:
  6.5 188.0 %copy-start = (bf16[128,128]{1,0:T(8,128)(2,1)S(1)}, bf16[128,128]{1,0:T(8,128)(2,1)}, u32[]{:S(2)}) copy-start(bf16[128,128]{1,0:T(8,128)(2,1)} %param.13) | copy-start | bytes 98308
  12.3 1.0 copy-start.3
  14.0 20.4 %copy-start.2 = (s32[64]{0:T(128)S(1)}, s32[64]{0:T(128)}, u32[]{:S(2)}) copy-start(s32[64]{0:T(128)} %param.11) | copy-start | bytes 772
  15.9 56.9 %all-to-all-start = ((bf16[1,1280,2,128]{3,2,0,1:T(2,128)(2,1)}), bf16[1,1280,2,128]{3,2,0,1:T(2,128)(2,1)S(1)}, u32[]{:S(2)}, u32[]{:S(2)}) async-start(bf16[1,1280,2,128]{3,2,0,1:T(2,128)(2,1)} %copy.34), calls=%async_computation | async-start | bytes 1310720 | tf_op jit(solution)/shard_map/all_to_all | solution.py:61
  72.8 81.8 %copy-start.1 = (f32[1280]{0:T(1024)S(1)}, f32[1280]{0:T(1024)}, u32[]{:S(2)}) copy-start(f32[1280]{0:T(1024)} %param.12) | copy-start | bytes 15364
  148.7 43.5 %all-to-all-start.1 = ((bf16[20,64,2,128]{3,2,0,1:T(2,128)(2,1)}), bf16[20,64,2,128]{3,2,0,1:T(2,128)(2,1)S(1)}, u32[]{:S(2)}, u32[]{:S(2)}) async-start(bf16[20,64,2,128]{3,2,0,1:T(2,128)(2,1)} %get-tuple-element.37), calls=%async_computation.1 | async-start | bytes 1310720 | tf_op jit(solution)/shard_map/all_to_all | solution.py:70
  154.6 78.4 %reduce-scatter.2.cloned.1.call-start = ((), (), s32[]{:S(2)}) async-start(), calls=%async_computation.3 | async-start | bytes 2949120 | tf_op jit(solution)/shard_map/reduce_scatter | solution.py:82
Sparse Core Ops, SparseCore 0:
  198.6 34.3 reduce-scatter.1
where the time goes:
time: 243 us; the launch traced here: 242 us
  waiting for transfers between devices  109 us (45%)
  local copies, waits for them, and re-layouts  42.4 us (17%)
  loops' own time  39.3 us (16%)
  starting transfers between devices  24.6 us (10%)
  between operations  13.6 us (6%)
  matrix products  9.64 us (4%)
  other arithmetic  3.19 us (1%)
    another operation x1, loops' own time, local(): returned = lax.map(per_latitude, jnp.arange(lat_local, dtype=jnp.int32))  39.3 us
    all_to_all x1, waiting for transfers between devices, local(): lax.all_to_all(returned, 'wave', split_axis=1, concat_axis=0, tiled=True)  37.4 us
    all_to_all x1, waiting for transfers between devices, local(): lax.all_to_all(at_lats, 'wave', split_axis=1, concat_axis=0, tiled=True)  37.2 us
    reduce_scatter x1, waiting for transfers between devices, local(): lax.psum_scatter(term.astype(jnp.bfloat16), 'lev', scatter_dimension=3, t...  34.5 us
    all_to_all x1, starting transfers between devices, local(): lax.all_to_all(at_lats, 'wave', split_axis=1, concat_axis=0, tiled=True)  18.6 us
    dynamic_update_slice x20, local copies, waits for them, and re-layouts, local(): returned = lax.map(per_latitude, jnp.arange(lat_local, dtype=jnp.int32))  13 us
    dynamic_slice x20, local copies, waits for them, and re-layouts, local(): returned = lax.map(per_latitude, jnp.arange(lat_local, dtype=jnp.int32))  12.1 us
    all_to_all x1, starting transfers between devices, local(): lax.all_to_all(returned, 'wave', split_axis=1, concat_axis=0, tiled=True)  5.92 us
  transfers between devices with their start and end apart: 3, of which 3 were waited for; matrix products, arithmetic and copies ran while one was open for 0% of the time, Pallas kernels for 0%

commit v1 on v0

v1 whole, which is shorter than its diff:
```python
import functools
import math

import jax
import jax.numpy as jnp
from jax import lax
from jax.experimental import pallas as pl
from jax.experimental.pallas import tpu as pltpu
from jax.sharding import Mesh
from jax.sharding import PartitionSpec as P

F = 8
TILE = 128
PEERS = ("y", "x", "z")
SIZES = {"z": 16, "x": 4, "y": 4, "core": 2}


def wave_tables(column_waves, lats, lon_count, wave_total):
    rows = wave_total * lats * 2
    longitudes = jnp.arange(lon_count, dtype=jnp.int32)
    phases = longitudes[:, None] * column_waves[None, :] % lon_count
    angles = phases.astype(jnp.float32) * (2.0 * math.pi / lon_count)
    imaginary = (jnp.arange(rows, dtype=jnp.int32) % 2 == 1)[None, :]
    basis = jnp.where(imaginary, -jnp.sin(angles), jnp.cos(angles))
    synthesis = (basis / math.sqrt(wave_total)).astype(jnp.bfloat16)
    phases_t = column_waves[:, None] * longitudes[None, :] % lon_count
    angles_t = phases_t.astype(jnp.float32) * (2.0 * math.pi / lon_count)
    basis_t = jnp.where(imaginary.T, -jnp.sin(angles_t), jnp.cos(angles_t))
    analysis = (basis_t / math.sqrt(lon_count)).astype(jnp.bfloat16)
    return synthesis, analysis


def grid_kernel(lats, received, synthesis, analysis, returned):
    blocks, rows, lanes = received.shape
    lon_count = synthesis.shape[0]
    column_lat = lax.broadcasted_iota(jnp.int32, (lon_count, rows), 1) // 2 % lats
    row_lat = lax.broadcasted_iota(jnp.int32, (rows, lon_count), 0) // 2 % lats
    step = 2
    for first in range(0, blocks, step):
        coeffs = jnp.concatenate([received[first + i] for i in range(step)], axis=1)
        width = step * lanes
        field_index = lax.broadcasted_iota(jnp.int32, (lon_count, width), 1) % F
        total = None
        for lat in range(lats):
            table = jnp.where(column_lat == lat, synthesis[...], jnp.zeros((), jnp.bfloat16))
            field = jnp.dot(table, coeffs, preferred_element_type=jnp.float32)
            following = pltpu.roll(field, width - 1, 1)
            wrapped = pltpu.roll(field, F - 1, 1)
            partner = jnp.where(field_index == F - 1, wrapped, following)
            product = (field * partner).astype(jnp.bfloat16)
            back = jnp.where(row_lat == lat, analysis[...], jnp.zeros((), jnp.bfloat16))
            term = jnp.dot(back, product, preferred_element_type=jnp.float32)
            total = term if total is None else total + term
        returned[:, first * lanes : (first + step) * lanes] = total.astype(jnp.bfloat16)


def couple_kernel(own, other, own_matrix, other_matrix, weight, sent):
    total = jnp.dot(own[...], own_matrix[...], preferred_element_type=jnp.float32)
    total += jnp.dot(other[...], other_matrix[...], preferred_element_type=jnp.float32)
    total *= weight[...]
    blocks, rows, lanes = sent.shape
    for i in range(blocks):
        sent[i] = total[:, i * lanes : (i + 1) * lanes].astype(jnp.bfloat16)


def call(kernel, out_shape, flops, limit, *operands):
    moved = sum(x.size * x.dtype.itemsize for x in operands) + out_shape.size * 2
    return pl.pallas_call(
        kernel,
        out_shape=out_shape,
        in_specs=[pl.BlockSpec(memory_space=pltpu.VMEM)] * len(operands),
        out_specs=pl.BlockSpec(memory_space=pltpu.VMEM),
        compiler_params=pltpu.CompilerParams(vmem_limit_bytes=limit << 20),
        cost_estimate=pl.CostEstimate(flops=flops, bytes_accessed=moved, transcendentals=0),
    )(*operands)


def local(spectral, legendre, pattern, assignment, quad_weight, coupling):
    degrees = spectral.shape[1]
    channels = spectral.shape[3]
    lat_count = legendre.shape[1]
    wave_total = assignment.shape[0]
    y_count = SIZES["y"]
    peers = y_count * wave_total
    lats = lat_count // peers
    rows = wave_total * lats * 2
    own_levels = channels // F
    slot = lax.axis_index("z") * SIZES["x"] + lax.axis_index("x")
    core = lax.axis_index("core")

    own_wave = lax.dynamic_index_in_dim(assignment, slot, 0, keepdims=False)
    own_mask = lax.dynamic_index_in_dim(pattern, own_wave, 0, keepdims=False).astype(jnp.bfloat16)
    lat_tiles, deg_tiles = own_mask.shape
    wide_mask = jnp.broadcast_to(
        own_mask[:, None, :, None], (lat_tiles, TILE, deg_tiles, TILE)
    ).reshape(lat_count, degrees)
    pruned = legendre[0] * wide_mask

    at_lats = jnp.einsum("ln,nch->lch", pruned, spectral[0], preferred_element_type=jnp.float32)
    at_lats = at_lats.astype(jnp.bfloat16).reshape(peers, lats, 2, channels)
    received = lax.all_to_all(at_lats, PEERS, split_axis=0, concat_axis=0, tiled=True)
    received = received.reshape(y_count, rows, channels)

    arrival = assignment.reshape(SIZES["z"], SIZES["x"]).T.reshape(wave_total)
    column_waves = jnp.broadcast_to(arrival[:, None], (wave_total, lats * 2)).reshape(rows)
    lon_count = 3 * wave_total
    synthesis, analysis = wave_tables(column_waves, lats, lon_count, wave_total)
    cores = SIZES["core"]
    split = coupling.reshape(y_count, cores, own_levels, y_count, cores, own_levels)
    mine = lax.dynamic_index_in_dim(split, core, 1, keepdims=False)
    wide = y_count * channels
    spread = (
        jnp.arange(wide, dtype=jnp.int32)[:, None] // F
        == jnp.arange(wide // F, dtype=jnp.int32)[None, :]
    ).astype(jnp.bfloat16)
    same_field = (
        jnp.arange(wide, dtype=jnp.int32)[:, None] % F
        == jnp.arange(wide, dtype=jnp.int32)[None, :] % F
    )

    def matrix(source):
        small = lax.dynamic_index_in_dim(mine, source, 3, keepdims=False)
        small = small.reshape(wide // F, wide // F)
        tall = jnp.einsum("pb,ab->pa", spread, small).astype(jnp.bfloat16)
        full = jnp.einsum("pa,qa->pq", tall, spread).astype(jnp.bfloat16)
        return jnp.where(same_field, full, jnp.zeros((), jnp.bfloat16))

    group = lax.axis_index(PEERS)
    weight = lax.dynamic_slice_in_dim(quad_weight, group * lats, lats)
    weight = jnp.broadcast_to(weight[None, :, None], (wave_total, lats, 2)).reshape(rows, 1)
    own_matrix, other_matrix = matrix(core), matrix(1 - core)
    received, synthesis, analysis, own_matrix, other_matrix, weight = lax.optimization_barrier(
        (received, synthesis, analysis, own_matrix, other_matrix, weight)
    )

    flops = 4 * lats * lon_count * rows * y_count * channels
    returned = call(
        functools.partial(grid_kernel, lats),
        jax.ShapeDtypeStruct((rows, y_count * channels), jnp.bfloat16),
        flops,
        16,
        received,
        synthesis,
        analysis,
    )
    swapped = lax.ppermute(returned, "core", [(0, 1), (1, 0)])

    sent = call(
        couple_kernel,
        jax.ShapeDtypeStruct((y_count, rows, channels), jnp.bfloat16),
        4 * rows * wide * wide,
        16,
        returned,
        swapped,
        own_matrix,
        other_matrix,
        weight,
    )
    sent = sent.reshape(peers, lats, 2, channels)
    weighted = lax.all_to_all(sent, PEERS, split_axis=0, concat_axis=0, tiled=True)
    weighted = weighted.reshape(lat_count, 2, channels)
    tendency = jnp.einsum("ln,lch->nch", pruned, weighted, preferred_element_type=jnp.float32)
    return tendency.astype(jnp.bfloat16)[None]


def solution(mesh):
    grid = Mesh(mesh.devices.reshape(tuple(SIZES.values())), tuple(SIZES))
    wave, lev = ("z", "x"), ("y", "core")
    placed = (P(wave, None, None, lev), P(wave, None, None), P(), P(), P(), P())
    return jax.shard_map(
        local,
        mesh=grid,
        in_specs=placed,
        out_specs=P(wave, None, None, lev),
        check_vma=False,
    )
```

time: 243 us -> 139 us (0.57)
  waiting for transfers between devices: 109 us -> 31.2 us
  blocking collectives: 0 us -> 48.9 us
  loops' own time: 39.3 us -> 0 us
  local copies, waits for them, and re-layouts: 42.4 us -> 16 us
  between operations: 13.6 us -> 2.16 us
  matrix products: 9.64 us -> 4.22 us
  Pallas kernels: 0 us -> 3.24 us
    all_to_all x0 -> x1, blocking collectives: none -> 48.9 us  [local(): lax.all_to_all(sent, PEERS, split_axis=0, concat_axis=0, tiled=True)]
    all_to_all x2 -> x1, waiting for transfers between devices: 74.5 us -> 29.3 us  [local(): lax.all_to_all(at_lats, PEERS, split_axis=0, concat_axis=0, tiled=True)]
    another operation x1 -> x0, loops' own time: 39.3 us -> none  [local(): returned = lax.map(per_latitude, jnp.arange(lat_local, dtype=jnp.int32))]
    reduce_scatter x1 -> x0, waiting for transfers between devices: 34.5 us -> none  [local(): lax.psum_scatter(term.astype(jnp.bfloat16), 'lev', scatter_dimension=3, t...]
    dynamic_update_slice x20 -> x0, local copies, waits for them, and re-layouts: 13 us -> none  [local(): returned = lax.map(per_latitude, jnp.arange(lat_local, dtype=jnp.int32))]
    dynamic_slice x41 -> x4, local copies, waits for them, and re-layouts: 13.9 us -> 3.79 us  [the longest x1 1.28 us: local(): own_wave = lax.dynamic_index_in_dim(assignment, slot, 0, keepdims=False)]
    dot_general x44 -> x4, matrix products: 9.64 us -> 4.22 us  [the longest x1 2.61 us: local(): jnp.einsum('ln,nch->lch', pruned, spectral[0], preferred_element_type=jnp...]
    convert_element_type x3, other arithmetic: 1.67 us -> 5.53 us  [the longest x1 3.34 us: wave_tables(): analysis = (basis_t / math.sqrt(lon_count)).astype(jnp.bfloat16)]
  transfers between devices with their start and end apart: 3 -> 2, of which waited for: 3 -> 2; matrix products, arithmetic and copies ran while one was open for 0% -> 7% of each run, Pallas kernels for 0% -> 0%
where the time goes in v1:
time: 139 us; the launch traced here: 137 us
  blocking collectives  48.9 us (35%)
  waiting for transfers between devices  31.2 us (22%)
  starting transfers between devices  25.6 us (18%)
  local copies, waits for them, and re-layouts  16 us (12%)
  other arithmetic  5.54 us (4%)
  matrix products  4.22 us (3%)
  Pallas kernels  3.24 us (2%)
  between operations  2.16 us (2%)
    all_to_all x1, blocking collectives, local(): lax.all_to_all(sent, PEERS, split_axis=0, concat_axis=0, tiled=True)  48.9 us
    all_to_all x1, waiting for transfers between devices, local(): lax.all_to_all(at_lats, PEERS, split_axis=0, concat_axis=0, tiled=True)  29.3 us
    all_to_all x1, starting transfers between devices, local(): lax.all_to_all(at_lats, PEERS, split_axis=0, concat_axis=0, tiled=True)  23.7 us
    convert_element_type x1, local copies, waits for them, and re-layouts, local(): at_lats = at_lats.astype(jnp.bfloat16).reshape(peers, lats, 2, channels)  6.2 us
    convert_element_type x1, other arithmetic, wave_tables(): analysis = (basis_t / math.sqrt(lon_count)).astype(jnp.bfloat16)  3.34 us
    pallas_call x2, Pallas kernels, call(): pl.pallas_call(kernel, out_shape=out_shape, in_specs=[pl.BlockSpec(memory...  3.24 us
    reshape x1, local copies, waits for them, and re-layouts, local(): wide_mask = jnp.broadcast_to(own_mask[:, None, :, None], (lat_tiles, TILE...  3.03 us
  transfers between devices with their start and end apart: 2, of which 2 were waited for; matrix products, arithmetic and copies ran while one was open for 7% of the time, Pallas kernels for 0%

profile of v1, /device:TPU:6, one launch (start us, length us, event | category | flops | bytes accessed | tf_op | source)
XLA Modules:
  0.0 136.9 jit_solution(12161466538159687350)
XLA Ops:
  0.0 1.3 dynamic_slice.20
  3.2 0.9 constant_dynamic-slice_fusion
  4.3 0.4 broadcast_in_dim.30
  4.8 3.0 %reshape.137 = bf16[1,1280,640]{2,1,0:T(8,128)(2,1)} reshape(bf16[10,128,5,128]{3,2,1,0:T(8,128)(2,1)S(1)} %broadcast_in_dim.30) | data formatting | bytes 3276800 | tf_op jit(solution)/shard_map/reshape | solution.py:96
  7.8 2.6 %convolution_convert_fusion = bf16[1280,2,128]{2,0,1:T(8,128)(2,1)S(1)} fusion(bf16[1,1280,640]{2,1,0:T(8,128)(2,1)} %param.7, bf16[1,1280,640]{2,1,0:T(8,128)(2,1)} %reshape.137, bf16[640,2,128]{2,1,0:T(2,128)(2,1)S(1)} %bitcast.25), kind=kOutput, calls=%fused_computation | convolution fusion | flops 423034880 | bytes 4259840 | tf_op jit(solution)/shard_map/ln,nch->lch/dot_general | solution.py:99
  10.4 6.2 %copy.18 = bf16[1280,2,128]{2,1,0:T(2,128)(2,1)} copy(bf16[1280,2,128]{2,0,1:T(8,128)(2,1)S(1)} %convolution_convert_fusion) | data formatting | bytes 1310720 | tf_op jit(solution)/shard_map/convert_element_type | solution.py:100
  16.6 23.7 %all-to-all-start = ((bf16[256,5,2,128]{3,2,1,0:T(2,128)(2,1)}), bf16[256,5,2,128]{3,2,1,0:T(2,128)(2,1)S(1)}, u32[]{:S(2)}, u32[]{:S(2)}) async-start(bf16[256,5,2,128]{3,2,1,0:T(2,128)(2,1)} %bitcast.6), calls=%async_computation | async-start | bytes 1310720 | tf_op jit(solution)/shard_map/all_to_all | solution.py:101
  40.5 0.2 reshape.141
  40.7 0.9 dynamic-slice_reduce_fusion
  41.8 0.8 dynamic_slice.24
  43.0 0.1 mul.63
  43.2 2.2 %multiply_convert_fusion.1.synthesis = bf16[192,640]{1,0:T(8,128)(2,1)S(1)} fusion(s32[640]{0:T(1024)S(1)} %mul.63, pred[640]{0:T(1024)(128)(4,1)S(1)} %fusion.31), kind=kLoop, calls=%fused_computation.24 | loop fusion | flops 1597440 | bytes 248960 | tf_op jit(solution)/shard_map/convert_element_type | solution.py:25
  45.4 3.3 %multiply_convert_fusion.analysis = bf16[640,192]{1,0:T(8,128)(2,1)S(1)} fusion(s32[640]{0:T(1024)S(1)} %mul.63, pred[640]{0:T(1024)(128)(4,1)S(1)} %fusion.31), kind=kLoop, calls=%fused_computation.15 | loop fusion | flops 1597440 | bytes 248960 | tf_op jit(solution)/shard_map/convert_element_type | solution.py:29
  48.8 0.5 compare_select_fusion.other_matrix
  49.2 0.5 compare_select_fusion.1.own_matrix
  49.7 29.3 %all-to-all-done = bf16[256,5,2,128]{3,2,1,0:T(2,128)(2,1)S(1)} async-done(((bf16[256,5,2,128]{3,2,1,0:T(2,128)(2,1)}), bf16[256,5,2,128]{3,2,1,0:T(2,128)(2,1)S(1)}, u32[]{:S(2)}, u32[]{:S(2)}) %all-to-all-start) | async-done | bytes 655392 | tf_op jit(solution)/shard_map/all_to_all | solution.py:101
  79.0 2.4 %shard_map.64.own = bf16[640,512]{1,0:T(8,128)(2,1)S(1)} custom-call(bf16[4,640,128]{2,1,0:T(8,128)(2,1)S(1)} %bitcast.27, bf16[192,640]{1,0:T(8,128)(2,1)S(1)} %multiply_convert_fusion.1.synthesis, bf16[640,192]{1,0:T(8,128)(2,1)S(1)} %multiply_convert_fusion.analysis), custom_call_target="tpu_custom_call" | custom-call | flops 1258291200 | bytes 1802240 | tf_op jit(solution)/shard_map/pallas_call | solution.py:68
  81.4 1.9 %collective-permute-start = (bf16[640,512]{1,0:T(8,128)(2,1)S(1)}, bf16[640,512]{1,0:T(8,128)(2,1)S(1)}, u32[]{:S(2)}, u32[]{:S(2)}) collective-permute-start(bf16[640,512]{1,0:T(8,128)(2,1)S(1)} %shard_map.64.own), channel_id=1, source_target_pairs={{0,1},{1,0},{2,3},{3,2},{4,5},{5,4},{6,7},{7,6},{8,9},{9,8},{10,11... | collective-permute-start | bytes 1966088 | tf_op jit(solution)/shard_map/ppermute | solution.py:146
  83.4 0.2 copy.22.weight
  83.6 1.9 %collective-permute-done.other = bf16[640,512]{1,0:T(8,128)(2,1)S(1)} collective-permute-done((bf16[640,512]{1,0:T(8,128)(2,1)S(1)}, bf16[640,512]{1,0:T(8,128)(2,1)S(1)}, u32[]{:S(2)}, u32[]{:S(2)}) %collective-permute-start) | collective-permute-done | bytes 655392 | tf_op jit(solution)/shard_map/ppermute | solution.py:146
  85.4 0.8 shard_map.65
  86.3 48.9 %all_to_all.10 = bf16[256,5,2,128]{3,2,1,0:T(2,128)(2,1)S(1)} all-to-all(bf16[256,5,2,128]{3,2,1,0:T(2,128)(2,1)S(1)} %bitcast.26), channel_id=1, replica_groups=mesh['z'=16,'x'=4,'y'=4,'core'=2] {'y','x','z'}, dimensions={0} | all-to-all | bytes 1310720 | tf_op jit(solution)/shard_map/all_to_all | solution.py:160
  135.2 0.7 fusion.6
  135.9 1.1 copy.25
  (23 shorter events, 1.0 us)
Async XLA Ops:
  0.0 7.8 %copy-start = (bf16[1,640,2,128]{3,2,1,0:T(2,128)(2,1)S(1)}, bf16[1,640,2,128]{3,2,1,0:T(2,128)(2,1)}, u32[]{:S(2)}) copy-start(bf16[1,640,2,128]{3,2,1,0:T(2,128)(2,1)} %param.6) | copy-start | bytes 983044
  10.4 30.0 %copy-start.3 = (s32[64]{0:T(128)S(1)}, s32[64]{0:T(128)}, u32[]{:S(2)}) copy-start(s32[64]{0:T(128)} %param.9) | copy-start | bytes 772
  10.4 30.0 %copy-start.2 = (bf16[128,128]{1,0:T(8,128)(2,1)S(1)}, bf16[128,128]{1,0:T(8,128)(2,1)}, u32[]{:S(2)}) copy-start(bf16[128,128]{1,0:T(8,128)(2,1)} %param.11) | copy-start | bytes 98308
  16.6 62.4 %all-to-all-start = ((bf16[256,5,2,128]{3,2,1,0:T(2,128)(2,1)}), bf16[256,5,2,128]{3,2,1,0:T(2,128)(2,1)S(1)}, u32[]{:S(2)}, u32[]{:S(2)}) async-start(bf16[256,5,2,128]{3,2,1,0:T(2,128)(2,1)} %bitcast.6), calls=%async_computation | async-start | bytes 1310720 | tf_op jit(solution)/shard_map/all_to_all | solution.py:101
  81.4 4.0 %collective-permute-start = (bf16[640,512]{1,0:T(8,128)(2,1)S(1)}, bf16[640,512]{1,0:T(8,128)(2,1)S(1)}, u32[]{:S(2)}, u32[]{:S(2)}) collective-permute-start(bf16[640,512]{1,0:T(8,128)(2,1)S(1)} %shard_map.64.own), channel_id=1, source_target_pairs={{0,1},{1,0},{2,3},{3,2},{4,5},{5,4},{6,7},{7,6},{8,9},{9,8},{10,11... | collective-permute-start | bytes 1966088 | tf_op jit(solution)/shard_map/ppermute | solution.py:146
  83.5 51.6 %copy-start.1 = (bf16[1,1280,640]{2,1,0:T(8,128)(2,1)S(1)}, bf16[1,1280,640]{2,1,0:T(8,128)(2,1)}, u32[]{:S(2)}) copy-start(bf16[1,1280,640]{2,1,0:T(8,128)(2,1)} %reshape.137) | copy-start | bytes 4915204
  83.6 51.6 %copy-start.4 = (bf16[1,1280,640]{2,1,0:T(8,128)(2,1)S(1)}, bf16[1,1280,640]{2,1,0:T(8,128)(2,1)}, u32[]{:S(2)}) copy-start(bf16[1,1280,640]{2,1,0:T(8,128)(2,1)} %param.7) | copy-start | bytes 4915204

commit v2 on v1

--- a/solution.py
+++ b/solution.py
@@ -11,6 +11,7 @@
 
 F = 8
 TILE = 128
+LAT_CHUNKS = 5
 PEERS = ("y", "x", "z")
 SIZES = {"z": 16, "x": 4, "y": 4, "core": 2}
 
@@ -28,6 +29,105 @@
     basis_t = jnp.where(imaginary.T, -jnp.sin(angles_t), jnp.cos(angles_t))
     analysis = (basis_t / math.sqrt(lon_count)).astype(jnp.bfloat16)
     return synthesis, analysis
+
+
+def even_odd(size):
+    row = lax.broadcasted_iota(jnp.int32, (size, 2 * size), 0)
+    column = lax.broadcasted_iota(jnp.int32, (size, 2 * size), 1)
+    return [(column == 2 * row + part).astype(jnp.bfloat16) for part in range(2)]
+
+
+def merge(size):
+    row = lax.broadcasted_iota(jnp.int32, (2 * size, 2 * size), 0)
+    column = lax.broadcasted_iota(jnp.int32, (2 * size, 2 * size), 1)
+    return (column == row % 2 * size + row // 2).astype(jnp.bfloat16)
+
+
+def forward_kernel(
+    spectral, legendre, pattern, assignment, at_lats, raw, matrix, coeffs, merged, in_sem, lat_sem, out_sem
+):
+    lat_tiles, deg_tiles, _ = pattern.shape
+    raw_copy = pltpu.make_async_copy(spectral, raw, in_sem)
+    raw_copy.start()
+    chunk = TILE * lat_tiles // LAT_CHUNKS
+
+    def lat_copy(i):
+        span = pl.ds(i * chunk, chunk)
+        return pltpu.make_async_copy(legendre.at[span], matrix.at[span], lat_sem.at[i])
+
+    for i in range(LAT_CHUNKS):
+        lat_copy(i).start()
+    slot = lax.axis_index("z") * SIZES["x"] + lax.axis_index("x")
+    wave = assignment[slot]
+    picked = lax.broadcasted_iota(jnp.int32, pattern.shape, 2) == wave
+    mask = jnp.sum(jnp.where(picked, pattern[...], 0), axis=2, keepdims=True)
+    halves = even_odd(TILE)
+    lanes = raw.shape[1]
+    raw_copy.wait()
+    for k in range(deg_tiles):
+        block = raw[2 * TILE * k : 2 * TILE * (k + 1), :]
+        for part in range(2):
+            coeffs[TILE * k : TILE * (k + 1), lanes * part : lanes * (part + 1)] = jnp.dot(
+                halves[part], block, preferred_element_type=jnp.float32
+            ).astype(jnp.bfloat16)
+    order = merge(TILE)
+
+    def out_copy(i):
+        span = pl.ds(2 * i * chunk, 2 * chunk)
+        return pltpu.make_async_copy(merged.at[span], at_lats.at[span], out_sem.at[i])
+
+    for i in range(LAT_CHUNKS):
+        lat_copy(i).wait()
+        for t in range(i * lat_tiles // LAT_CHUNKS, (i + 1) * lat_tiles // LAT_CHUNKS):
+            keep = jnp.concatenate(
+                [
+                    jnp.broadcast_to(mask[t, k : k + 1, :], (TILE, TILE)).astype(jnp.bfloat16)
+                    for k in range(deg_tiles)
+                ],
+                axis=1,
+            )
+            pruned = matrix[TILE * t : TILE * (t + 1), :] * keep
+            found = jnp.dot(pruned, coeffs[...], preferred_element_type=jnp.float32)
+            found = found.astype(jnp.bfloat16)
+            stacked = jnp.concatenate([found[:, :lanes], found[:, lanes:]], axis=0)
+            merged[2 * TILE * t : 2 * TILE * (t + 1), :] = jnp.dot(
+                order, stacked, preferred_element_type=jnp.float32
+            ).astype(jnp.bfloat16)
+        out_copy(i).start()
+    for i in range(LAT_CHUNKS):
+        out_copy(i).wait()
+
+
+def forward(spectral, legendre, pattern, assignment):
+    degrees, _, channels = spectral.shape
+    lat_count = legendre.shape[0]
+    anywhere = pl.BlockSpec(memory_space=pl.ANY)
+    return pl.pallas_call(
+        forward_kernel,
+        out_shape=jax.ShapeDtypeStruct((2 * lat_count, channels), jnp.bfloat16),
+        in_specs=[
+            anywhere,
+            anywhere,
+            pl.BlockSpec(memory_space=pltpu.VMEM),
+            pl.BlockSpec(memory_space=pltpu.SMEM),
+        ],
+        out_specs=anywhere,
+        scratch_shapes=[
+            pltpu.VMEM((2 * degrees, channels), jnp.bfloat16),
+            pltpu.VMEM((lat_count, degrees), jnp.bfloat16),
+            pltpu.VMEM((degrees, 2 * channels), jnp.bfloat16),
+            pltpu.VMEM((2 * lat_count, channels), jnp.bfloat16),
+            pltpu.SemaphoreType.DMA,
+            pltpu.SemaphoreType.DMA((LAT_CHUNKS,)),
+            pltpu.SemaphoreType.DMA((LAT_CHUNKS,)),
+        ],
+        compiler_params=pltpu.CompilerParams(vmem_limit_bytes=16 << 20),
+    )(
+        spectral.reshape(2 * degrees, channels),
+        legendre,
+        jnp.transpose(pattern, (1, 2, 0)),
+        assignment,
+    )
 
 
 def grid_kernel(lats, received, synthesis, analysis, returned):
@@ -96,8 +196,8 @@
     ).reshape(lat_count, degrees)
     pruned = legendre[0] * wide_mask
 
-    at_lats = jnp.einsum("ln,nch->lch", pruned, spectral[0], preferred_element_type=jnp.float32)
-    at_lats = at_lats.astype(jnp.bfloat16).reshape(peers, lats, 2, channels)
+    at_lats = forward(spectral[0], legendre[0], pattern, assignment)
+    at_lats = at_lats.reshape(peers, lats, 2, channels)
     received = lax.all_to_all(at_lats, PEERS, split_axis=0, concat_axis=0, tiled=True)
     received = received.reshape(y_count, rows, channels)
 
@@ -129,8 +229,10 @@
     weight = lax.dynamic_slice_in_dim(quad_weight, group * lats, lats)
     weight = jnp.broadcast_to(weight[None, :, None], (wave_total, lats, 2)).reshape(rows, 1)
     own_matrix, other_matrix = matrix(core), matrix(1 - core)
-    received, synthesis, analysis, own_matrix, other_matrix, weight = lax.optimization_barrier(
-        (received, synthesis, analysis, own_matrix, other_matrix, weight)
+    received, synthesis, analysis, own_matrix, other_matrix, weight, pruned = (
+        lax.optimization_barrier(
+            (received, synthesis, analysis, own_matrix, other_matrix, weight, pruned)
+        )
     )
 
     flops = 4 * lats * lon_count * rows * y_count * channels

time: 139 us -> 134 us (0.964)
  waiting for transfers between devices: 31.2 us -> 24.5 us
  Pallas kernels: 3.24 us -> 9.15 us
  local copies, waits for them, and re-layouts: 16 us -> 11.6 us
  other arithmetic: 5.54 us -> 8.33 us
  matrix products: 4.22 us -> 1.58 us
    all_to_all x1, waiting for transfers between devices: 29.3 us -> 22.7 us  [local(): lax.all_to_all(at_lats, PEERS, split_axis=0, concat_axis=0, tiled=True)]
    unnamed x11 -> x23, local copies, waits for them, and re-layouts: 0.16 us -> 6.44 us
    convert_element_type x1 -> x0, local copies, waits for them, and re-layouts: 6.2 us -> none  [local(): at_lats = at_lats.astype(jnp.bfloat16).reshape(peers, lats, 2, channels)]
    pallas_call x0 -> x1, Pallas kernels: none -> 5.97 us  [forward(): pl.pallas_call(forward_kernel, out_shape=jax.ShapeDtypeStruct((2 * lat_co...]
    reshape x1 -> x0, local copies, waits for them, and re-layouts: 3.03 us -> none  [local(): wide_mask = jnp.broadcast_to(own_mask[:, None, :, None], (lat_tiles, TILE...]
    dot_general x1 -> x0, matrix products: 2.61 us -> none  [local(): jnp.einsum('ln,nch->lch', pruned, spectral[0], preferred_element_type=jnp...]
    mul x0 -> x1, other arithmetic: none -> 1.49 us  [local(): pruned = legendre[0] * wide_mask]
  transfers between devices with their start and end apart: 2 -> 2, of which waited for: 2 -> 2; matrix products, arithmetic and copies ran while one was open for 7% -> 10% of each run, Pallas kernels for 0% -> 0%
where the time goes in v2:
time: 134 us; the launch traced here: 132 us
  blocking collectives  49 us (37%)
  starting transfers between devices  25.7 us (19%)
  waiting for transfers between devices  24.5 us (18%)
  local copies, waits for them, and re-layouts  11.6 us (9%)
  Pallas kernels  9.15 us (7%)
  other arithmetic  8.33 us (6%)
  between operations  2.17 us (2%)
  matrix products  1.58 us (1%)
    all_to_all x1, blocking collectives, local(): lax.all_to_all(sent, PEERS, split_axis=0, concat_axis=0, tiled=True)  49 us
    all_to_all x1, starting transfers between devices, local(): lax.all_to_all(at_lats, PEERS, split_axis=0, concat_axis=0, tiled=True)  23.7 us
    all_to_all x1, waiting for transfers between devices, local(): lax.all_to_all(at_lats, PEERS, split_axis=0, concat_axis=0, tiled=True)  22.7 us
    unnamed x23, local copies, waits for them, and re-layouts  6.44 us
    pallas_call x1, Pallas kernels, forward(): pl.pallas_call(forward_kernel, out_shape=jax.ShapeDtypeStruct((2 * lat_co...  5.97 us
    convert_element_type x1, other arithmetic, wave_tables(): analysis = (basis_t / math.sqrt(lon_count)).astype(jnp.bfloat16)  3.94 us
    pallas_call x2, Pallas kernels, call(): pl.pallas_call(kernel, out_shape=out_shape, in_specs=[pl.BlockSpec(memory...  3.18 us
    convert_element_type x1, other arithmetic, wave_tables(): synthesis = (basis / math.sqrt(wave_total)).astype(jnp.bfloat16)  2.89 us
  transfers between devices with their start and end apart: 2, of which 2 were waited for; matrix products, arithmetic and copies ran while one was open for 10% of the time, Pallas kernels for 0%

profile of v2, /device:TPU:6, one launch (start us, length us, event | category | flops | bytes accessed | tf_op | source)
XLA Modules:
  0.0 132.0 jit_solution(13281254543148039615)
XLA Ops:
  0.0 1.4 %copy-done = bf16[1,1280,640]{2,1,0:T(8,128)(2,1)S(1)} copy-done((bf16[1,1280,640]{2,1,0:T(8,128)(2,1)S(1)}, bf16[1,1280,640]{2,1,0:T(8,128)(2,1)}, u32[]{:S(2)}) %copy-start) | copy-done | bytes 1638424
  1.4 1.0 copy-done.2
  2.4 0.8 copy-done.3
  3.2 0.7 copy-done.5
  3.8 6.0 %shard_map.64 = bf16[2560,128]{1,0:T(8,128)(2,1)} custom-call(bf16[1280,128]{1,0:T(8,128)(2,1)S(1)} %bitcast.30, bf16[1280,640]{1,0:T(8,128)(2,1)S(1)} %bitcast.27, s32[10,5,64]{2,1,0:T(8,128)S(1)} %bitcast.31, s32[64]{0:T(128)S(1)} %copy-done.5), custom_call_target="tpu_custom_call" | custom-call | tf_op jit(solution)/shard_map/pallas_call | solution.py:105
  9.8 23.7 %all-to-all-start = ((bf16[256,5,2,128]{3,2,1,0:T(2,128)(2,1)}), bf16[256,5,2,128]{3,2,1,0:T(2,128)(2,1)S(1)}, u32[]{:S(2)}, u32[]{:S(2)}) async-start(bf16[256,5,2,128]{3,2,1,0:T(2,128)(2,1)} %bitcast.3), calls=%async_computation | async-start | bytes 1310720 | tf_op jit(solution)/shard_map/all_to_all | solution.py:201
  33.6 0.6 dynamic_slice.23
  36.8 0.9 dynamic-slice_reduce_fusion
  37.9 0.8 dynamic_slice.22
  39.3 2.9 %multiply_convert_fusion.1.synthesis = bf16[192,640]{1,0:T(8,128)(2,1)} fusion(s32[640]{0:T(1024)S(1)} %mul.56, pred[640]{0:T(1024)(128)(4,1)S(1)} %fusion.27), kind=kLoop, calls=%fused_computation.21 | loop fusion | flops 1597440 | bytes 248960 | tf_op jit(solution)/shard_map/convert_element_type | solution.py:26
  42.2 3.9 %multiply_convert_fusion.analysis = bf16[640,192]{1,0:T(8,128)(2,1)} fusion(s32[640]{0:T(1024)S(1)} %mul.56, pred[640]{0:T(1024)(128)(4,1)S(1)} %fusion.27), kind=kLoop, calls=%fused_computation.14 | loop fusion | flops 1597440 | bytes 248960 | tf_op jit(solution)/shard_map/convert_element_type | solution.py:30
  46.6 0.5 compare_select_fusion.1.own_matrix
  47.5 0.5 copy-done.1
  48.0 1.5 %bitcast_multiply_fusion = bf16[1280,640]{1,0:T(8,128)(2,1)} fusion(bf16[160,8,5,128]{3,2,1,0:T(8,128)(2,1)S(1)} %bitcast.32, bf16[1,1280,640]{2,1,0:T(8,128)(2,1)S(1)} %copy-done.1), kind=kLoop, calls=%fused_computation | loop fusion | flops 819200 | bytes 4915200 | tf_op jit(solution)/shard_map/mul | solution.py:197
  49.5 22.7 %all-to-all-done = bf16[256,5,2,128]{3,2,1,0:T(2,128)(2,1)S(1)} async-done(((bf16[256,5,2,128]{3,2,1,0:T(2,128)(2,1)}), bf16[256,5,2,128]{3,2,1,0:T(2,128)(2,1)S(1)}, u32[]{:S(2)}, u32[]{:S(2)}) %all-to-all-start) | async-done | bytes 655392 | tf_op jit(solution)/shard_map/all_to_all | solution.py:201
  72.2 1.0 copy-done.7
  73.2 0.9 copy-done.8
  74.1 2.3 %shard_map.65.own = bf16[640,512]{1,0:T(8,128)(2,1)S(1)} custom-call(bf16[4,640,128]{2,1,0:T(8,128)(2,1)S(1)} %bitcast.29, bf16[192,640]{1,0:T(8,128)(2,1)S(1)} %copy-done.8, bf16[640,192]{1,0:T(8,128)(2,1)S(1)} %copy-done.7), custom_call_target="tpu_custom_call" | custom-call | flops 1258291200 | bytes 1802240 | tf_op jit(solution)/shard_map/pallas_call | solution.py:168
  76.5 1.9 %collective-permute-start = (bf16[640,512]{1,0:T(8,128)(2,1)S(1)}, bf16[640,512]{1,0:T(8,128)(2,1)S(1)}, u32[]{:S(2)}, u32[]{:S(2)}) collective-permute-start(bf16[640,512]{1,0:T(8,128)(2,1)S(1)} %shard_map.65.own), channel_id=1, source_target_pairs={{0,1},{1,0},{2,3},{3,2},{4,5},{5,4},{6,7},{7,6},{8,9},{9,8},{10,11... | collective-permute-start | bytes 1966088 | tf_op jit(solution)/shard_map/ppermute | solution.py:248
  78.6 1.9 %collective-permute-done.other = bf16[640,512]{1,0:T(8,128)(2,1)S(1)} collective-permute-done((bf16[640,512]{1,0:T(8,128)(2,1)S(1)}, bf16[640,512]{1,0:T(8,128)(2,1)S(1)}, u32[]{:S(2)}, u32[]{:S(2)}) %collective-permute-start) | collective-permute-done | bytes 655392 | tf_op jit(solution)/shard_map/ppermute | solution.py:248
  80.4 0.8 shard_map.66
  81.3 49.0 %all_to_all.10 = bf16[256,5,2,128]{3,2,1,0:T(2,128)(2,1)S(1)} all-to-all(bf16[256,5,2,128]{3,2,1,0:T(2,128)(2,1)S(1)} %bitcast.28), channel_id=1, replica_groups=mesh['z'=16,'x'=4,'y'=4,'core'=2] {'y','x','z'}, dimensions={0} | all-to-all | bytes 1310720 | tf_op jit(solution)/shard_map/all_to_all | solution.py:262
  130.3 0.6 fusion.5
  130.9 1.1 copy.21
  (34 shorter events, 2.5 us)
Async XLA Ops:
  0.0 1.4 %copy-start = (bf16[1,1280,640]{2,1,0:T(8,128)(2,1)S(1)}, bf16[1,1280,640]{2,1,0:T(8,128)(2,1)}, u32[]{:S(2)}) copy-start(bf16[1,1280,640]{2,1,0:T(8,128)(2,1)} %param.7) | copy-start | bytes 4915204
  1.4 1.0 copy-start.2
  2.4 0.8 copy-start.3
  3.2 0.7 copy-start.5
  3.8 29.7 %copy-start.6 = (s32[64]{0:T(128)S(1)}, s32[64]{0:T(128)}, u32[]{:S(2)}) copy-start(s32[64]{0:T(128)} %assignment.1) | copy-start | bytes 772
  3.8 32.4 %copy-start.4 = (s32[64,10,5]{0,2,1:T(8,128)S(1)}, s32[64,10,5]{0,2,1:T(8,128)}, u32[]{:S(2)}) copy-start(s32[64,10,5]{0,2,1:T(8,128)} %param.8) | copy-start | bytes 38404
  3.8 32.7 %copy-start.10 = (bf16[128,128]{1,0:T(8,128)(2,1)S(1)}, bf16[128,128]{1,0:T(8,128)(2,1)}, u32[]{:S(2)}) copy-start(bf16[128,128]{1,0:T(8,128)(2,1)} %param.11) | copy-start | bytes 98308
  9.8 62.4 %all-to-all-start = ((bf16[256,5,2,128]{3,2,1,0:T(2,128)(2,1)}), bf16[256,5,2,128]{3,2,1,0:T(2,128)(2,1)S(1)}, u32[]{:S(2)}, u32[]{:S(2)}) async-start(bf16[256,5,2,128]{3,2,1,0:T(2,128)(2,1)} %bitcast.3), calls=%async_computation | async-start | bytes 1310720 | tf_op jit(solution)/shard_map/all_to_all | solution.py:201
  46.6 1.4 %copy-start.1 = (bf16[1,1280,640]{2,1,0:T(8,128)(2,1)S(1)}, bf16[1,1280,640]{2,1,0:T(8,128)(2,1)}, u32[]{:S(2)}) copy-start(bf16[1,1280,640]{2,1,0:T(8,128)(2,1)} %param.7) | copy-start | bytes 4915204
  72.2 1.0 copy-start.7
  73.2 0.9 copy-start.8
  76.5 4.0 %collective-permute-start = (bf16[640,512]{1,0:T(8,128)(2,1)S(1)}, bf16[640,512]{1,0:T(8,128)(2,1)S(1)}, u32[]{:S(2)}, u32[]{:S(2)}) collective-permute-start(bf16[640,512]{1,0:T(8,128)(2,1)S(1)} %shard_map.65.own), channel_id=1, source_target_pairs={{0,1},{1,0},{2,3},{3,2},{4,5},{5,4},{6,7},{7,6},{8,9},{9,8},{10,11... | collective-permute-start | bytes 1966088 | tf_op jit(solution)/shard_map/ppermute | solution.py:248
  78.6 51.7 %copy-start.9 = (bf16[1280,640]{1,0:T(8,128)(2,1)S(1)}, bf16[1280,640]{1,0:T(8,128)(2,1)}, u32[]{:S(2)}) copy-start(bf16[1280,640]{1,0:T(8,128)(2,1)} %bitcast_multiply_fusion) | copy-start | bytes 4915204

commit v3 on v1

--- a/solution.py
+++ b/solution.py
@@ -11,47 +11,143 @@
 
 F = 8
 TILE = 128
+LAT_CHUNKS = 2
 PEERS = ("y", "x", "z")
 SIZES = {"z": 16, "x": 4, "y": 4, "core": 2}
 
 
-def wave_tables(column_waves, lats, lon_count, wave_total):
-    rows = wave_total * lats * 2
+def wave_tables(waves, lon_count):
+    wave_total = waves.shape[0]
     longitudes = jnp.arange(lon_count, dtype=jnp.int32)
-    phases = longitudes[:, None] * column_waves[None, :] % lon_count
+    phases = longitudes[:, None] * waves[None, :] % lon_count
     angles = phases.astype(jnp.float32) * (2.0 * math.pi / lon_count)
-    imaginary = (jnp.arange(rows, dtype=jnp.int32) % 2 == 1)[None, :]
-    basis = jnp.where(imaginary, -jnp.sin(angles), jnp.cos(angles))
+    basis = jnp.concatenate([jnp.cos(angles), -jnp.sin(angles)], axis=1)
     synthesis = (basis / math.sqrt(wave_total)).astype(jnp.bfloat16)
-    phases_t = column_waves[:, None] * longitudes[None, :] % lon_count
-    angles_t = phases_t.astype(jnp.float32) * (2.0 * math.pi / lon_count)
-    basis_t = jnp.where(imaginary.T, -jnp.sin(angles_t), jnp.cos(angles_t))
-    analysis = (basis_t / math.sqrt(lon_count)).astype(jnp.bfloat16)
+    analysis = (basis.T / math.sqrt(lon_count)).astype(jnp.bfloat16)
     return synthesis, analysis
 
 
-def grid_kernel(lats, received, synthesis, analysis, returned):
+def forward_kernel(
+    spectral, legendre, pattern, assignment, at_lats,
+    raw, matrix, blocks, waves, paired, coeffs, wide, merged, in_sem, lat_sem, out_sem,
+):
+    lat_tiles, deg_tiles, _ = pattern.shape
+    lat_count, degrees = legendre.shape
+    lanes = raw.shape[1]
+    chunk = lat_count // LAT_CHUNKS
+    copies = [
+        pltpu.make_async_copy(source, target, in_sem.at[i])
+        for i, (source, target) in enumerate(
+            ((spectral, raw), (assignment, waves), (pattern, blocks))
+        )
+    ]
+    for copy in copies:
+        copy.start()
+
+    def lat_copy(i):
+        span = pl.ds(i * chunk, chunk)
+        return pltpu.make_async_copy(legendre.at[span], matrix.at[span], lat_sem.at[i])
+
+    def out_copy(i):
+        span = pl.ds(2 * i * chunk, 2 * chunk)
+        return pltpu.make_async_copy(merged.at[span], at_lats.at[span], out_sem.at[i])
+
+    for i in range(LAT_CHUNKS):
+        lat_copy(i).start()
+    copies[0].wait()
+    paired[...] = raw[...].astype(jnp.float32)
+    for part in range(2):
+        coeffs[:, part * lanes : (part + 1) * lanes] = paired[
+            pl.ds(part, degrees, stride=2), :
+        ].astype(jnp.bfloat16)
+    copies[1].wait()
+    copies[2].wait()
+    slot = lax.axis_index("z") * SIZES["x"] + lax.axis_index("x")
+    wave = waves[slot]
+    picked = lax.broadcasted_iota(jnp.int32, blocks.shape, 2) == wave
+    mask = jnp.sum(jnp.where(picked, blocks[...], 0), axis=2, keepdims=True)
+    for i in range(LAT_CHUNKS):
+        lat_copy(i).wait()
+        for t in range(i * lat_tiles // LAT_CHUNKS, (i + 1) * lat_tiles // LAT_CHUNKS):
+            keep = jnp.concatenate(
+                [
+                    jnp.broadcast_to(mask[t, k : k + 1, :], (TILE, TILE)).astype(jnp.bfloat16)
+                    for k in range(deg_tiles)
+                ],
+                axis=1,
+            )
+            tile = slice(TILE * t, TILE * (t + 1))
+            matrix[tile, :] = matrix[tile, :] * keep
+        found = jnp.dot(
+            matrix[chunk * i : chunk * (i + 1), :],
+            coeffs[...],
+            preferred_element_type=jnp.float32,
+        )
+        for part in range(2):
+            wide[pl.ds(part, chunk, stride=2), :] = found[:, part * lanes : (part + 1) * lanes]
+        merged[2 * chunk * i : 2 * chunk * (i + 1), :] = wide[...].astype(jnp.bfloat16)
+        out_copy(i).start()
+    for i in range(LAT_CHUNKS):
+        out_copy(i).wait()
+
+
+def forward(spectral, legendre, pattern, assignment):
+    degrees, _, channels = spectral.shape
+    lat_count = legendre.shape[0]
+    pattern = jnp.transpose(pattern, (1, 2, 0))
+    chunk = lat_count // LAT_CHUNKS
+    return pl.pallas_call(
+        forward_kernel,
+        out_shape=jax.ShapeDtypeStruct((2 * lat_count, channels), jnp.bfloat16),
+        in_specs=[pl.BlockSpec(memory_space=pltpu.HBM)] * 4,
+        out_specs=pl.BlockSpec(memory_space=pltpu.HBM),
+        scratch_shapes=[
+            pltpu.VMEM((2 * degrees, channels), jnp.bfloat16),
+            pltpu.VMEM((lat_count, degrees), jnp.bfloat16),
+            pltpu.VMEM(pattern.shape, jnp.int32),
+            pltpu.SMEM(assignment.shape, jnp.int32),
+            pltpu.VMEM((2 * degrees, channels), jnp.float32),
+            pltpu.VMEM((degrees, 2 * channels), jnp.bfloat16),
+            pltpu.VMEM((2 * chunk, channels), jnp.float32),
+            pltpu.VMEM((2 * lat_count, channels), jnp.bfloat16),
+            pltpu.SemaphoreType.DMA((3,)),
+            pltpu.SemaphoreType.DMA((LAT_CHUNKS,)),
+            pltpu.SemaphoreType.DMA((LAT_CHUNKS,)),
+        ],
+        compiler_params=pltpu.CompilerParams(vmem_limit_bytes=16 << 20),
+    )(spectral.reshape(2 * degrees, channels), legendre, pattern, assignment)
+
+
+def grid_kernel(lats, received, synthesis, analysis, returned, wide):
     blocks, rows, lanes = received.shape
-    lon_count = synthesis.shape[0]
-    column_lat = lax.broadcasted_iota(jnp.int32, (lon_count, rows), 1) // 2 % lats
-    row_lat = lax.broadcasted_iota(jnp.int32, (rows, lon_count), 0) // 2 % lats
-    step = 2
-    for first in range(0, blocks, step):
-        coeffs = jnp.concatenate([received[first + i] for i in range(step)], axis=1)
-        width = step * lanes
-        field_index = lax.broadcasted_iota(jnp.int32, (lon_count, width), 1) % F
-        total = None
-        for lat in range(lats):
-            table = jnp.where(column_lat == lat, synthesis[...], jnp.zeros((), jnp.bfloat16))
-            field = jnp.dot(table, coeffs, preferred_element_type=jnp.float32)
-            following = pltpu.roll(field, width - 1, 1)
-            wrapped = pltpu.roll(field, F - 1, 1)
-            partner = jnp.where(field_index == F - 1, wrapped, following)
-            product = (field * partner).astype(jnp.bfloat16)
-            back = jnp.where(row_lat == lat, analysis[...], jnp.zeros((), jnp.bfloat16))
-            term = jnp.dot(back, product, preferred_element_type=jnp.float32)
-            total = term if total is None else total + term
-        returned[:, first * lanes : (first + step) * lanes] = total.astype(jnp.bfloat16)
+    width = blocks * lanes
+    slots = rows // (2 * lats)
+    wide[...] = received[...].astype(jnp.float32)
+    last_field = lax.broadcasted_iota(jnp.int32, (synthesis.shape[0], width), 1) % F == F - 1
+
+    def span(lat, part):
+        return pl.ds(2 * lat + part, slots, stride=2 * lats)
+
+    for lat in range(lats):
+        coeffs = jnp.concatenate(
+            [
+                jnp.concatenate([wide[i, span(lat, part), :] for i in range(blocks)], axis=1)
+                for part in range(2)
+            ],
+            axis=0,
+        ).astype(jnp.bfloat16)
+        field = jnp.dot(synthesis[...], coeffs, preferred_element_type=jnp.float32)
+        following = pltpu.roll(field, width - 1, 1)
+        wrapped = pltpu.roll(field, F - 1, 1)
+        product = (field * jnp.where(last_field, wrapped, following)).astype(jnp.bfloat16)
+        back = jnp.dot(analysis[...], product, preferred_element_type=jnp.float32)
+        for part in range(2):
+            for i in range(blocks):
+                wide[i, span(lat, part), :] = back[
+                    part * slots : (part + 1) * slots, i * lanes : (i + 1) * lanes
+                ]
+    for i in range(blocks):
+        returned[:, i * lanes : (i + 1) * lanes] = wide[i].astype(jnp.bfloat16)
 
 
 def couple_kernel(own, other, own_matrix, other_matrix, weight, sent):
@@ -63,13 +159,14 @@
         sent[i] = total[:, i * lanes : (i + 1) * lanes].astype(jnp.bfloat16)
 
 
-def call(kernel, out_shape, flops, limit, *operands):
+def call(kernel, out_shape, flops, limit, *operands, scratch=()):
     moved = sum(x.size * x.dtype.itemsize for x in operands) + out_shape.size * 2
     return pl.pallas_call(
         kernel,
         out_shape=out_shape,
         in_specs=[pl.BlockSpec(memory_space=pltpu.VMEM)] * len(operands),
         out_specs=pl.BlockSpec(memory_space=pltpu.VMEM),
+        scratch_shapes=scratch,
         compiler_params=pltpu.CompilerParams(vmem_limit_bytes=limit << 20),
         cost_estimate=pl.CostEstimate(flops=flops, bytes_accessed=moved, transcendentals=0),
     )(*operands)
@@ -96,15 +193,14 @@
     ).reshape(lat_count, degrees)
     pruned = legendre[0] * wide_mask
 
-    at_lats = jnp.einsum("ln,nch->lch", pruned, spectral[0], preferred_element_type=jnp.float32)
-    at_lats = at_lats.astype(jnp.bfloat16).reshape(peers, lats, 2, channels)
+    at_lats = forward(spectral[0], legendre[0], pattern, assignment)
+    at_lats = at_lats.reshape(peers, lats, 2, channels)
     received = lax.all_to_all(at_lats, PEERS, split_axis=0, concat_axis=0, tiled=True)
     received = received.reshape(y_count, rows, channels)
 
     arrival = assignment.reshape(SIZES["z"], SIZES["x"]).T.reshape(wave_total)
-    column_waves = jnp.broadcast_to(arrival[:, None], (wave_total, lats * 2)).reshape(rows)
     lon_count = 3 * wave_total
-    synthesis, analysis = wave_tables(column_waves, lats, lon_count, wave_total)
+    synthesis, analysis = wave_tables(arrival, lon_count)
     cores = SIZES["core"]
     split = coupling.reshape(y_count, cores, own_levels, y_count, cores, own_levels)
     mine = lax.dynamic_index_in_dim(split, core, 1, keepdims=False)
@@ -129,19 +225,23 @@
     weight = lax.dynamic_slice_in_dim(quad_weight, group * lats, lats)
     weight = jnp.broadcast_to(weight[None, :, None], (wave_total, lats, 2)).reshape(rows, 1)
     own_matrix, other_matrix = matrix(core), matrix(1 - core)
-    received, synthesis, analysis, own_matrix, other_matrix, weight = lax.optimization_barrier(
-        (received, synthesis, analysis, own_matrix, other_matrix, weight)
-    )
-
-    flops = 4 * lats * lon_count * rows * y_count * channels
+    received, synthesis, analysis, own_matrix, other_matrix, weight, pruned = (
+        lax.optimization_barrier(
+            (received, synthesis, analysis, own_matrix, other_matrix, weight, pruned)
+        )
+    )
+
+    wide = y_count * channels
+    flops = 4 * lon_count * rows * wide
     returned = call(
         functools.partial(grid_kernel, lats),
-        jax.ShapeDtypeStruct((rows, y_count * channels), jnp.bfloat16),
+        jax.ShapeDtypeStruct((rows, wide), jnp.bfloat16),
         flops,
         16,
         received,
         synthesis,
         analysis,
+        scratch=[pltpu.VMEM((y_count, rows, channels), jnp.float32)],
     )
     swapped = lax.ppermute(returned, "core", [(0, 1), (1, 0)])
 

time: 139 us -> 130 us (0.935)
  local copies, waits for them, and re-layouts: 16 us -> 9.56 us
  other arithmetic: 5.54 us -> 1.88 us
  Pallas kernels: 3.24 us -> 6.36 us
  matrix products: 4.22 us -> 1.58 us
    convert_element_type x1 -> x0, local copies, waits for them, and re-layouts: 6.2 us -> none  [local(): at_lats = at_lats.astype(jnp.bfloat16).reshape(peers, lats, 2, channels)]
    convert_element_type x2 -> x1, other arithmetic: 5.53 us -> 0.02 us  [wave_tables(): analysis = (basis.T / math.sqrt(lon_count)).astype(jnp.bfloat16)]
    unnamed x11 -> x19, local copies, waits for them, and re-layouts: 0.16 us -> 4.52 us
    reshape x1 -> x0, local copies, waits for them, and re-layouts: 3.03 us -> none  [local(): wide_mask = jnp.broadcast_to(own_mask[:, None, :, None], (lat_tiles, TILE...]
    pallas_call x0 -> x1, Pallas kernels: none -> 3.02 us  [forward(): pl.pallas_call(forward_kernel, out_shape=jax.ShapeDtypeStruct((2 * lat_co...]
    dot_general x1 -> x0, matrix products: 2.61 us -> none  [local(): jnp.einsum('ln,nch->lch', pruned, spectral[0], preferred_element_type=jnp...]
    mul x0 -> x1, other arithmetic: none -> 1.49 us  [local(): pruned = legendre[0] * wide_mask]
  transfers between devices with their start and end apart: 2 -> 2, of which waited for: 2 -> 2; matrix products, arithmetic and copies ran while one was open for 7% -> 5% of each run, Pallas kernels for 0% -> 0%
where the time goes in v3:
time: 130 us; the launch traced here: 128 us
  blocking collectives  49.1 us (38%)
  waiting for transfers between devices  31.2 us (24%)
  starting transfers between devices  25.6 us (20%)
  local copies, waits for them, and re-layouts  9.56 us (7%)
  Pallas kernels  6.36 us (5%)
  between operations  2.17 us (2%)
  other arithmetic  1.88 us (1%)
  matrix products  1.58 us (1%)
    all_to_all x1, blocking collectives, local(): lax.all_to_all(sent, PEERS, split_axis=0, concat_axis=0, tiled=True)  49.1 us
    all_to_all x1, waiting for transfers between devices, local(): lax.all_to_all(at_lats, PEERS, split_axis=0, concat_axis=0, tiled=True)  29.3 us
    all_to_all x1, starting transfers between devices, local(): lax.all_to_all(at_lats, PEERS, split_axis=0, concat_axis=0, tiled=True)  23.7 us
    unnamed x19, local copies, waits for them, and re-layouts  4.52 us
    pallas_call x2, Pallas kernels, call(): pl.pallas_call(kernel, out_shape=out_shape, in_specs=[pl.BlockSpec(memory...  3.34 us
    pallas_call x1, Pallas kernels, forward(): pl.pallas_call(forward_kernel, out_shape=jax.ShapeDtypeStruct((2 * lat_co...  3.02 us
  transfers between devices with their start and end apart: 2, of which 2 were waited for; matrix products, arithmetic and copies ran while one was open for 5% of the time, Pallas kernels for 0%

profile of v3, /device:TPU:6, one launch (start us, length us, event | category | flops | bytes accessed | tf_op | source)
XLA Modules:
  0.0 127.6 jit_solution(3303919310334404257)
XLA Ops:
  0.0 1.4 %copy-done = bf16[1,1280,640]{2,1,0:T(8,128)(2,1)S(1)} copy-done((bf16[1,1280,640]{2,1,0:T(8,128)(2,1)S(1)}, bf16[1,1280,640]{2,1,0:T(8,128)(2,1)}, u32[]{:S(2)}) %copy-start) | copy-done | bytes 1638424
  1.4 1.0 copy-done.2
  2.4 0.8 copy-done.3
  3.2 0.7 copy-done.5
  3.8 3.0 %shard_map.64 = bf16[2560,128]{1,0:T(8,128)(2,1)} custom-call(bf16[1280,128]{1,0:T(8,128)(2,1)S(1)} %bitcast.32, bf16[1280,640]{1,0:T(8,128)(2,1)S(1)} %bitcast.29, s32[10,5,64]{2,1,0:T(8,128)S(1)} %bitcast.33, s32[64]{0:T(128)S(1)} %copy-done.5), custom_call_target="tpu_custom_call" | custom-call | tf_op jit(solution)/shard_map/pallas_call | solution.py:99
  6.9 23.7 %all-to-all-start = ((bf16[256,5,2,128]{3,2,1,0:T(2,128)(2,1)}), bf16[256,5,2,128]{3,2,1,0:T(2,128)(2,1)S(1)}, u32[]{:S(2)}, u32[]{:S(2)}) async-start(bf16[256,5,2,128]{3,2,1,0:T(2,128)(2,1)} %bitcast.3), calls=%async_computation | async-start | bytes 1310720 | tf_op jit(solution)/shard_map/all_to_all | solution.py:198
  30.6 0.6 dynamic_slice.23
  33.6 0.2 reshape.114
  33.8 0.9 dynamic-slice_reduce_fusion
  34.9 0.8 dynamic_slice.22
  36.1 0.4 fusion.22
  36.5 0.5 compare_select_fusion.other_matrix
  37.0 0.5 compare_select_fusion.1.own_matrix
  37.5 0.4 broadcast_in_dim.12
  37.9 0.5 copy-done.1
  38.4 1.5 %bitcast_multiply_fusion = bf16[1280,640]{1,0:T(8,128)(2,1)} fusion(bf16[160,8,5,128]{3,2,1,0:T(8,128)(2,1)S(1)} %bitcast.34, bf16[1,1280,640]{2,1,0:T(8,128)(2,1)S(1)} %copy-done.1), kind=kLoop, calls=%fused_computation | loop fusion | flops 819200 | bytes 4915200 | tf_op jit(solution)/shard_map/mul | solution.py:194
  39.9 29.3 %all-to-all-done = bf16[256,5,2,128]{3,2,1,0:T(2,128)(2,1)S(1)} async-done(((bf16[256,5,2,128]{3,2,1,0:T(2,128)(2,1)}), bf16[256,5,2,128]{3,2,1,0:T(2,128)(2,1)S(1)}, u32[]{:S(2)}, u32[]{:S(2)}) %all-to-all-start) | async-done | bytes 655392 | tf_op jit(solution)/shard_map/all_to_all | solution.py:198
  69.4 2.5 %shard_map.65.own = bf16[640,512]{1,0:T(8,128)(2,1)S(1)} custom-call(bf16[4,640,128]{2,1,0:T(8,128)(2,1)S(1)} %bitcast.31, bf16[192,128]{1,0:T(8,128)(2,1)S(1)} %copy.19.synthesis, bf16[128,192]{1,0:T(8,128)(2,1)S(1)} %get-tuple-element.15.analysis), custom_call_target="tpu_custom_call" | custom-call | flops 251658240 | bytes 1409024 | tf_op jit(solution)/shard_map/pallas_call | solution.py:164
  71.9 1.9 %collective-permute-start = (bf16[640,512]{1,0:T(8,128)(2,1)S(1)}, bf16[640,512]{1,0:T(8,128)(2,1)S(1)}, u32[]{:S(2)}, u32[]{:S(2)}) collective-permute-start(bf16[640,512]{1,0:T(8,128)(2,1)S(1)} %shard_map.65.own), channel_id=1, source_target_pairs={{0,1},{1,0},{2,3},{3,2},{4,5},{5,4},{6,7},{7,6},{8,9},{9,8},{10,11... | collective-permute-start | bytes 1966088 | tf_op jit(solution)/shard_map/ppermute | solution.py:246
  74.0 1.9 %collective-permute-done.other = bf16[640,512]{1,0:T(8,128)(2,1)S(1)} collective-permute-done((bf16[640,512]{1,0:T(8,128)(2,1)S(1)}, bf16[640,512]{1,0:T(8,128)(2,1)S(1)}, u32[]{:S(2)}, u32[]{:S(2)}) %collective-permute-start) | collective-permute-done | bytes 655392 | tf_op jit(solution)/shard_map/ppermute | solution.py:246
  75.9 0.8 shard_map.66
  76.7 49.1 %all_to_all.10 = bf16[256,5,2,128]{3,2,1,0:T(2,128)(2,1)S(1)} all-to-all(bf16[256,5,2,128]{3,2,1,0:T(2,128)(2,1)S(1)} %bitcast.30), channel_id=1, replica_groups=mesh['z'=16,'x'=4,'y'=4,'core'=2] {'y','x','z'}, dimensions={0} | all-to-all | bytes 1310720 | tf_op jit(solution)/shard_map/all_to_all | solution.py:260
  125.9 0.6 fusion.5
  126.5 1.1 copy.23
  (28 shorter events, 1.3 us)
Async XLA Ops:
  0.0 1.4 %copy-start = (bf16[1,1280,640]{2,1,0:T(8,128)(2,1)S(1)}, bf16[1,1280,640]{2,1,0:T(8,128)(2,1)}, u32[]{:S(2)}) copy-start(bf16[1,1280,640]{2,1,0:T(8,128)(2,1)} %param.7) | copy-start | bytes 4915204
  1.4 1.0 copy-start.2
  2.4 0.8 copy-start.3
  3.2 0.7 copy-start.5
  3.8 26.8 %copy-start.6 = (s32[64]{0:T(128)S(1)}, s32[64]{0:T(128)}, u32[]{:S(2)}) copy-start(s32[64]{0:T(128)} %assignment.1) | copy-start | bytes 772
  3.8 29.4 %copy-start.4 = (s32[64,10,5]{0,2,1:T(8,128)S(1)}, s32[64,10,5]{0,2,1:T(8,128)}, u32[]{:S(2)}) copy-start(s32[64,10,5]{0,2,1:T(8,128)} %param.8) | copy-start | bytes 38404
  3.8 29.7 %copy-start.8 = (bf16[128,128]{1,0:T(8,128)(2,1)S(1)}, bf16[128,128]{1,0:T(8,128)(2,1)}, u32[]{:S(2)}) copy-start(bf16[128,128]{1,0:T(8,128)(2,1)} %param.11) | copy-start | bytes 98308
  6.9 62.4 %all-to-all-start = ((bf16[256,5,2,128]{3,2,1,0:T(2,128)(2,1)}), bf16[256,5,2,128]{3,2,1,0:T(2,128)(2,1)S(1)}, u32[]{:S(2)}, u32[]{:S(2)}) async-start(bf16[256,5,2,128]{3,2,1,0:T(2,128)(2,1)} %bitcast.3), calls=%async_computation | async-start | bytes 1310720 | tf_op jit(solution)/shard_map/all_to_all | solution.py:198
  37.0 1.4 %copy-start.1 = (bf16[1,1280,640]{2,1,0:T(8,128)(2,1)S(1)}, bf16[1,1280,640]{2,1,0:T(8,128)(2,1)}, u32[]{:S(2)}) copy-start(bf16[1,1280,640]{2,1,0:T(8,128)(2,1)} %param.7) | copy-start | bytes 4915204
  71.9 4.0 %collective-permute-start = (bf16[640,512]{1,0:T(8,128)(2,1)S(1)}, bf16[640,512]{1,0:T(8,128)(2,1)S(1)}, u32[]{:S(2)}, u32[]{:S(2)}) collective-permute-start(bf16[640,512]{1,0:T(8,128)(2,1)S(1)} %shard_map.65.own), channel_id=1, source_target_pairs={{0,1},{1,0},{2,3},{3,2},{4,5},{5,4},{6,7},{7,6},{8,9},{9,8},{10,11... | collective-permute-start | bytes 1966088 | tf_op jit(solution)/shard_map/ppermute | solution.py:246
  74.0 51.9 %copy-start.7 = (bf16[1280,640]{1,0:T(8,128)(2,1)S(1)}, bf16[1280,640]{1,0:T(8,128)(2,1)}, u32[]{:S(2)}) copy-start(bf16[1280,640]{1,0:T(8,128)(2,1)} %bitcast_multiply_fusion) | copy-start | bytes 4915204

commit v4 on v3

--- a/solution.py
+++ b/solution.py
@@ -114,32 +114,40 @@
             pltpu.SemaphoreType.DMA((LAT_CHUNKS,)),
             pltpu.SemaphoreType.DMA((LAT_CHUNKS,)),
         ],
-        compiler_params=pltpu.CompilerParams(vmem_limit_bytes=16 << 20),
     )(spectral.reshape(2 * degrees, channels), legendre, pattern, assignment)
 
 
-def grid_kernel(lats, received, synthesis, analysis, returned, wide):
+def grid_kernel(lats, received, synthesis, analysis, returned, wide, ahead):
     blocks, rows, lanes = received.shape
     width = blocks * lanes
     slots = rows // (2 * lats)
     wide[...] = received[...].astype(jnp.float32)
-    last_field = lax.broadcasted_iota(jnp.int32, (synthesis.shape[0], width), 1) % F == F - 1
+    pair = 2 * lanes
+    source = lax.broadcasted_iota(jnp.int32, (pair, pair), 0)
+    target = lax.broadcasted_iota(jnp.int32, (pair, pair), 1)
+    advance = (source == target // F * F + (target + 1) % F).astype(jnp.bfloat16)
+    for i in range(0, blocks, 2):
+        both = jnp.concatenate([received[i], received[i + 1]], axis=1)
+        moved = jnp.dot(both, advance, preferred_element_type=jnp.float32)
+        ahead[i] = moved[:, :lanes]
+        ahead[i + 1] = moved[:, lanes:]
 
     def span(lat, part):
         return pl.ds(2 * lat + part, slots, stride=2 * lats)
 
+    def gather(rows_of, lat):
+        parts = [
+            jnp.concatenate([rows_of[i, span(lat, part), :] for i in range(blocks)], axis=1)
+            for part in range(2)
+        ]
+        return jnp.concatenate(parts, axis=0).astype(jnp.bfloat16)
+
     for lat in range(lats):
-        coeffs = jnp.concatenate(
-            [
-                jnp.concatenate([wide[i, span(lat, part), :] for i in range(blocks)], axis=1)
-                for part in range(2)
-            ],
-            axis=0,
-        ).astype(jnp.bfloat16)
-        field = jnp.dot(synthesis[...], coeffs, preferred_element_type=jnp.float32)
-        following = pltpu.roll(field, width - 1, 1)
-        wrapped = pltpu.roll(field, F - 1, 1)
-        product = (field * jnp.where(last_field, wrapped, following)).astype(jnp.bfloat16)
+        field, partner = (
+            jnp.dot(synthesis[...], gather(rows_of, lat), preferred_element_type=jnp.float32)
+            for rows_of in (wide, ahead)
+        )
+        product = (field * partner).astype(jnp.bfloat16)
         back = jnp.dot(analysis[...], product, preferred_element_type=jnp.float32)
         for part in range(2):
             for i in range(blocks):
@@ -241,7 +249,7 @@
         received,
         synthesis,
         analysis,
-        scratch=[pltpu.VMEM((y_count, rows, channels), jnp.float32)],
+        scratch=[pltpu.VMEM((y_count, rows, channels), jnp.float32)] * 2,
     )
     swapped = lax.ppermute(returned, "core", [(0, 1), (1, 0)])
 

time: 130 us -> 126 us (0.969)
  local copies, waits for them, and re-layouts: 9.56 us -> 6.21 us
    unnamed x19 -> x11, local copies, waits for them, and re-layouts: 4.52 us -> 1.16 us
  transfers between devices with their start and end apart: 2 -> 2, of which waited for: 2 -> 2; matrix products, arithmetic and copies ran while one was open for 5% -> 6% of each run, Pallas kernels for 0% -> 0%
where the time goes in v4:
time: 126 us; the launch traced here: 123 us
  blocking collectives  49 us (39%)
  waiting for transfers between devices  30.8 us (24%)
  starting transfers between devices  25.6 us (20%)
  Pallas kernels  6.28 us (5%)
  local copies, waits for them, and re-layouts  6.21 us (5%)
  between operations  2.17 us (2%)
  other arithmetic  1.86 us (1%)
  matrix products  1.58 us (1%)
    all_to_all x1, blocking collectives, local(): lax.all_to_all(sent, PEERS, split_axis=0, concat_axis=0, tiled=True)  49 us
    all_to_all x1, waiting for transfers between devices, local(): lax.all_to_all(at_lats, PEERS, split_axis=0, concat_axis=0, tiled=True)  28.9 us
    all_to_all x1, starting transfers between devices, local(): lax.all_to_all(at_lats, PEERS, split_axis=0, concat_axis=0, tiled=True)  23.7 us
    pallas_call x1, Pallas kernels, forward(): pl.pallas_call(forward_kernel, out_shape=jax.ShapeDtypeStruct((2 * lat_co...  3.56 us
    pallas_call x2, Pallas kernels, call(): pl.pallas_call(kernel, out_shape=out_shape, in_specs=[pl.BlockSpec(memory...  2.72 us
  transfers between devices with their start and end apart: 2, of which 2 were waited for; matrix products, arithmetic and copies ran while one was open for 6% of the time, Pallas kernels for 0%

profile of v4, /device:TPU:6, one launch (start us, length us, event | category | flops | bytes accessed | tf_op | source)
XLA Modules:
  0.0 123.5 jit_solution(15391833153223234956)
XLA Ops:
  0.0 3.6 %shard_map.64 = bf16[2560,128]{1,0:T(8,128)(2,1)} custom-call(bf16[1280,128]{1,0:T(8,128)(2,1)} %bitcast.35, bf16[1280,640]{1,0:T(8,128)(2,1)} %bitcast.32, s32[10,5,64]{2,1,0:T(8,128)} %bitcast.36, s32[64]{0:T(128)} %assignment.1), custom_call_target="tpu_custom_call" | custom-call | tf_op jit(solution)/shard_map/pallas_call | solution.py:99
  3.6 23.7 %all-to-all-start = ((bf16[256,5,2,128]{3,2,1,0:T(2,128)(2,1)}), bf16[256,5,2,128]{3,2,1,0:T(2,128)(2,1)S(1)}, u32[]{:S(2)}, u32[]{:S(2)}) async-start(bf16[256,5,2,128]{3,2,1,0:T(2,128)(2,1)} %bitcast.33), calls=%async_computation | async-start | bytes 1310720 | tf_op jit(solution)/shard_map/all_to_all | solution.py:206
  27.3 0.6 dynamic_slice.23
  30.1 0.1 copy.28
  30.3 0.2 reshape.114
  30.5 0.9 dynamic-slice_reduce_fusion
  31.6 0.8 dynamic_slice.22
  32.5 0.1 reshape.117
  32.8 0.4 fusion.22
  33.2 0.5 compare_select_fusion.other_matrix
  33.7 0.5 compare_select_fusion.1.own_matrix
  34.2 0.4 broadcast_in_dim.12
  34.6 1.0 copy-done
  35.6 1.5 %bitcast_multiply_fusion = bf16[1280,640]{1,0:T(8,128)(2,1)} fusion(bf16[160,8,5,128]{3,2,1,0:T(8,128)(2,1)S(1)} %bitcast.31, bf16[1,1280,640]{2,1,0:T(8,128)(2,1)S(1)} %copy-done), kind=kLoop, calls=%fused_computation | loop fusion | flops 819200 | bytes 4915200 | tf_op jit(solution)/shard_map/mul | solution.py:202
  37.1 28.9 %all-to-all-done = bf16[256,5,2,128]{3,2,1,0:T(2,128)(2,1)S(1)} async-done(((bf16[256,5,2,128]{3,2,1,0:T(2,128)(2,1)}), bf16[256,5,2,128]{3,2,1,0:T(2,128)(2,1)S(1)}, u32[]{:S(2)}, u32[]{:S(2)}) %all-to-all-start) | async-done | bytes 655392 | tf_op jit(solution)/shard_map/all_to_all | solution.py:206
  65.9 0.1 copy.19.synthesis
  66.1 1.9 %shard_map.65.own = bf16[640,512]{1,0:T(8,128)(2,1)S(1)} custom-call(bf16[4,640,128]{2,1,0:T(8,128)(2,1)S(1)} %bitcast.30, bf16[192,128]{1,0:T(8,128)(2,1)S(1)} %copy.19.synthesis, bf16[128,192]{1,0:T(8,128)(2,1)S(1)} %get-tuple-element.15.analysis), custom_call_target="tpu_custom_call" | custom-call | flops 251658240 | bytes 1409024 | tf_op jit(solution)/shard_map/pallas_call | solution.py:172
  67.9 1.9 %collective-permute-start = (bf16[640,512]{1,0:T(8,128)(2,1)S(1)}, bf16[640,512]{1,0:T(8,128)(2,1)S(1)}, u32[]{:S(2)}, u32[]{:S(2)}) collective-permute-start(bf16[640,512]{1,0:T(8,128)(2,1)S(1)} %shard_map.65.own), channel_id=1, source_target_pairs={{0,1},{1,0},{2,3},{3,2},{4,5},{5,4},{6,7},{7,6},{8,9},{9,8},{10,11... | collective-permute-start | bytes 1966088 | tf_op jit(solution)/shard_map/ppermute | solution.py:254
  69.9 0.2 copy.20.weight
  70.1 1.9 %collective-permute-done.other = bf16[640,512]{1,0:T(8,128)(2,1)S(1)} collective-permute-done((bf16[640,512]{1,0:T(8,128)(2,1)S(1)}, bf16[640,512]{1,0:T(8,128)(2,1)S(1)}, u32[]{:S(2)}, u32[]{:S(2)}) %collective-permute-start) | collective-permute-done | bytes 655392 | tf_op jit(solution)/shard_map/ppermute | solution.py:254
  71.9 0.8 shard_map.66
  72.8 49.0 %all_to_all.10 = bf16[256,5,2,128]{3,2,1,0:T(2,128)(2,1)S(1)} all-to-all(bf16[256,5,2,128]{3,2,1,0:T(2,128)(2,1)S(1)} %bitcast.29), channel_id=1, replica_groups=mesh['z'=16,'x'=4,'y'=4,'core'=2] {'y','x','z'}, dimensions={0} | all-to-all | bytes 1310720 | tf_op jit(solution)/shard_map/all_to_all | solution.py:268
  121.8 0.6 fusion.5
  122.4 1.1 copy.23
  (20 shorter events, 0.8 us)
Async XLA Ops:
  0.0 27.3 %copy-start.4 = (s32[64]{0:T(128)S(1)}, s32[64]{0:T(128)}, u32[]{:S(2)}) copy-start(s32[64]{0:T(128)} %assignment.1) | copy-start | bytes 772
  0.0 30.0 %copy-start.2 = (s32[64,10,5]{0,2,1:T(8,128)S(1)}, s32[64,10,5]{0,2,1:T(8,128)}, u32[]{:S(2)}) copy-start(s32[64,10,5]{0,2,1:T(8,128)} %param.8) | copy-start | bytes 38404
  0.0 30.3 %copy-start.3 = (bf16[128,128]{1,0:T(8,128)(2,1)S(1)}, bf16[128,128]{1,0:T(8,128)(2,1)}, u32[]{:S(2)}) copy-start(bf16[128,128]{1,0:T(8,128)(2,1)} %param.11) | copy-start | bytes 98308
  3.6 62.4 %all-to-all-start = ((bf16[256,5,2,128]{3,2,1,0:T(2,128)(2,1)}), bf16[256,5,2,128]{3,2,1,0:T(2,128)(2,1)S(1)}, u32[]{:S(2)}, u32[]{:S(2)}) async-start(bf16[256,5,2,128]{3,2,1,0:T(2,128)(2,1)} %bitcast.33), calls=%async_computation | async-start | bytes 1310720 | tf_op jit(solution)/shard_map/all_to_all | solution.py:206
  34.2 1.4 %copy-start = (bf16[1,1280,640]{2,1,0:T(8,128)(2,1)S(1)}, bf16[1,1280,640]{2,1,0:T(8,128)(2,1)}, u32[]{:S(2)}) copy-start(bf16[1,1280,640]{2,1,0:T(8,128)(2,1)} %param.7) | copy-start | bytes 4915204
  67.9 4.0 %collective-permute-start = (bf16[640,512]{1,0:T(8,128)(2,1)S(1)}, bf16[640,512]{1,0:T(8,128)(2,1)S(1)}, u32[]{:S(2)}, u32[]{:S(2)}) collective-permute-start(bf16[640,512]{1,0:T(8,128)(2,1)S(1)} %shard_map.65.own), channel_id=1, source_target_pairs={{0,1},{1,0},{2,3},{3,2},{4,5},{5,4},{6,7},{7,6},{8,9},{9,8},{10,11... | collective-permute-start | bytes 1966088 | tf_op jit(solution)/shard_map/ppermute | solution.py:254
  70.0 51.7 %copy-start.1 = (bf16[1280,640]{1,0:T(8,128)(2,1)S(1)}, bf16[1280,640]{1,0:T(8,128)(2,1)}, u32[]{:S(2)}) copy-start(bf16[1280,640]{1,0:T(8,128)(2,1)} %bitcast_multiply_fusion) | copy-start | bytes 4915204

commit v5 on v4

--- a/solution.py
+++ b/solution.py
@@ -14,6 +14,44 @@
 LAT_CHUNKS = 2
 PEERS = ("y", "x", "z")
 SIZES = {"z": 16, "x": 4, "y": 4, "core": 2}
+
+
+def middle(axis):
+    return SIZES[axis] // 2
+
+
+def peer_groups():
+    order = [
+        [(place + middle(axis)) % SIZES[axis] for place in range(SIZES[axis])] for axis in PEERS
+    ]
+    return [
+        [
+            ((z * SIZES["x"] + x) * SIZES["y"] + y) * SIZES["core"] + core
+            for y in order[0]
+            for x in order[1]
+            for z in order[2]
+        ]
+        for core in range(SIZES["core"])
+    ]
+
+
+def own_position():
+    position = 0
+    for axis in PEERS:
+        place = lax.rem(lax.axis_index(axis) + middle(axis), SIZES[axis])
+        position = position * SIZES[axis] + place
+    return position
+
+
+def exchange(values):
+    return lax.all_to_all(
+        values,
+        tuple(SIZES),
+        split_axis=0,
+        concat_axis=0,
+        axis_index_groups=peer_groups(),
+        tiled=True,
+    )
 
 
 def wave_tables(waves, lon_count):
@@ -203,14 +241,16 @@
 
     at_lats = forward(spectral[0], legendre[0], pattern, assignment)
     at_lats = at_lats.reshape(peers, lats, 2, channels)
-    received = lax.all_to_all(at_lats, PEERS, split_axis=0, concat_axis=0, tiled=True)
+    received = exchange(at_lats)
     received = received.reshape(y_count, rows, channels)
 
-    arrival = assignment.reshape(SIZES["z"], SIZES["x"]).T.reshape(wave_total)
+    arrival = assignment.reshape(SIZES["z"], SIZES["x"])
+    arrival = jnp.roll(arrival, (-middle("z"), -middle("x")), (0, 1)).T.reshape(wave_total)
     lon_count = 3 * wave_total
     synthesis, analysis = wave_tables(arrival, lon_count)
     cores = SIZES["core"]
     split = coupling.reshape(y_count, cores, own_levels, y_count, cores, own_levels)
+    split = jnp.roll(split, (-middle("y"), -middle("y")), (0, 3))
     mine = lax.dynamic_index_in_dim(split, core, 1, keepdims=False)
     wide = y_count * channels
     spread = (
@@ -229,7 +269,7 @@
         full = jnp.einsum("pa,qa->pq", tall, spread).astype(jnp.bfloat16)
         return jnp.where(same_field, full, jnp.zeros((), jnp.bfloat16))
 
-    group = lax.axis_index(PEERS)
+    group = own_position()
     weight = lax.dynamic_slice_in_dim(quad_weight, group * lats, lats)
     weight = jnp.broadcast_to(weight[None, :, None], (wave_total, lats, 2)).reshape(rows, 1)
     own_matrix, other_matrix = matrix(core), matrix(1 - core)
@@ -265,7 +305,7 @@
         weight,
     )
     sent = sent.reshape(peers, lats, 2, channels)
-    weighted = lax.all_to_all(sent, PEERS, split_axis=0, concat_axis=0, tiled=True)
+    weighted = exchange(sent)
     weighted = weighted.reshape(lat_count, 2, channels)
     tendency = jnp.einsum("ln,lch->nch", pruned, weighted, preferred_element_type=jnp.float32)
     return tendency.astype(jnp.bfloat16)[None]

time: 126 us -> 117 us (0.929); the launches traced: 123 us -> 117 us
  waiting for transfers between devices: 30.8 us -> 21.2 us
  starting transfers between devices: 25.6 us -> 28.8 us
    all_to_all x1, waiting for transfers between devices: 28.9 us -> 19.3 us  [exchange(): lax.all_to_all(values, tuple(SIZES), split_axis=0, concat_axis=0, axis_in...]
    all_to_all x1, starting transfers between devices: 23.7 us -> 26.9 us  [exchange(): lax.all_to_all(values, tuple(SIZES), split_axis=0, concat_axis=0, axis_in...]
where the time goes in v5:
time: 117 us
  blocking collectives  48.9 us (42%)
  starting transfers between devices  28.8 us (25%)
  waiting for transfers between devices  21.2 us (18%)
  Pallas kernels  6.24 us (5%)
  local copies, waits for them, and re-layouts  5.91 us (5%)
  between operations  2.2 us (2%)
  other arithmetic  2.16 us (2%)
  matrix products  1.75 us (1%)
    all_to_all x1, blocking collectives, exchange(): lax.all_to_all(values, tuple(SIZES), split_axis=0, concat_axis=0, axis_in...  48.9 us
    all_to_all x1, starting transfers between devices, exchange(): lax.all_to_all(values, tuple(SIZES), split_axis=0, concat_axis=0, axis_in...  26.9 us
    all_to_all x1, waiting for transfers between devices, exchange(): lax.all_to_all(values, tuple(SIZES), split_axis=0, concat_axis=0, axis_in...  19.3 us
    pallas_call x1, Pallas kernels, forward(): pl.pallas_call(forward_kernel, out_shape=jax.ShapeDtypeStruct((2 * lat_co...  3.51 us
    pallas_call x2, Pallas kernels, call(): pl.pallas_call(kernel, out_shape=out_shape, in_specs=[pl.BlockSpec(memory...  2.72 us
  transfers between devices with their start and end apart: 2, of which 2 were waited for; matrix products, arithmetic and copies ran while one was open for 6% of the time, Pallas kernels for 0%

profile of v5, /device:TPU:6, one launch (start us, length us, event | category | flops | bytes accessed | tf_op | source)
XLA Modules:
  0.0 117.1 jit_solution(11905601297554311610)
XLA Ops:
  0.0 3.5 %shard_map.64 = bf16[2560,128]{1,0:T(8,128)(2,1)} custom-call(bf16[1280,128]{1,0:T(8,128)(2,1)} %bitcast.40, bf16[1280,640]{1,0:T(8,128)(2,1)} %bitcast.37, s32[10,5,64]{2,1,0:T(8,128)} %bitcast.41, s32[64]{0:T(128)} %assignment.1), custom_call_target="tpu_custom_call" | custom-call | tf_op jit(solution)/shard_map/pallas_call | solution.py:137
  3.5 26.9 %all-to-all-start = ((bf16[256,5,2,128]{3,2,1,0:T(2,128)(2,1)}), bf16[256,5,2,128]{3,2,1,0:T(2,128)(2,1)S(1)}, u32[]{:S(2)}, u32[]{:S(2)}) async-start(bf16[256,5,2,128]{3,2,1,0:T(2,128)(2,1)} %bitcast.38), calls=%async_computation | async-start | bytes 1310720 | tf_op jit(solution)/shard_map/all_to_all | solution.py:47
  30.4 0.6 dynamic_slice.23
  33.0 0.1 copy.37
  33.2 0.1 slice.67
  33.6 0.8 dynamic_slice.22
  34.5 0.1 reshape.131
  34.7 0.2 fusion.31
  34.9 0.2 fusion.18
  35.9 0.4 fusion.24
  36.3 0.6 compare_select_fusion.other_matrix
  36.9 0.6 compare_select_fusion.1.own_matrix
  37.4 0.4 broadcast_in_dim.12
  37.8 1.0 copy-done
  38.9 1.5 %bitcast_multiply_fusion = bf16[1280,640]{1,0:T(8,128)(2,1)} fusion(bf16[160,8,5,128]{3,2,1,0:T(8,128)(2,1)S(1)} %bitcast.36, bf16[1,1280,640]{2,1,0:T(8,128)(2,1)S(1)} %copy-done), kind=kLoop, calls=%fused_computation | loop fusion | flops 819200 | bytes 4915200 | tf_op jit(solution)/shard_map/mul | solution.py:240
  40.4 19.3 %all-to-all-done = bf16[256,5,2,128]{3,2,1,0:T(2,128)(2,1)S(1)} async-done(((bf16[256,5,2,128]{3,2,1,0:T(2,128)(2,1)}), bf16[256,5,2,128]{3,2,1,0:T(2,128)(2,1)S(1)}, u32[]{:S(2)}, u32[]{:S(2)}) %all-to-all-start) | async-done | bytes 655392 | tf_op jit(solution)/shard_map/all_to_all | solution.py:47
  59.8 1.9 %shard_map.65.own = bf16[640,512]{1,0:T(8,128)(2,1)S(1)} custom-call(bf16[4,640,128]{2,1,0:T(8,128)(2,1)S(1)} %bitcast.35, bf16[192,128]{1,0:T(8,128)(2,1)S(1)} %copy.30.synthesis, bf16[128,192]{1,0:T(8,128)(2,1)S(1)} %get-tuple-element.15.analysis), custom_call_target="tpu_custom_call" | custom-call | flops 251658240 | bytes 1409024 | tf_op jit(solution)/shard_map/pallas_call | solution.py:210
  61.7 1.9 %collective-permute-start = (bf16[640,512]{1,0:T(8,128)(2,1)S(1)}, bf16[640,512]{1,0:T(8,128)(2,1)S(1)}, u32[]{:S(2)}, u32[]{:S(2)}) collective-permute-start(bf16[640,512]{1,0:T(8,128)(2,1)S(1)} %shard_map.65.own), channel_id=1, source_target_pairs={{0,1},{1,0},{2,3},{3,2},{4,5},{5,4},{6,7},{7,6},{8,9},{9,8},{10,11... | collective-permute-start | bytes 1966088 | tf_op jit(solution)/shard_map/ppermute | solution.py:294
  63.6 0.2 copy.31.weight
  63.8 1.9 %collective-permute-done.other = bf16[640,512]{1,0:T(8,128)(2,1)S(1)} collective-permute-done((bf16[640,512]{1,0:T(8,128)(2,1)S(1)}, bf16[640,512]{1,0:T(8,128)(2,1)S(1)}, u32[]{:S(2)}, u32[]{:S(2)}) %collective-permute-start) | collective-permute-done | bytes 655392 | tf_op jit(solution)/shard_map/ppermute | solution.py:294
  65.7 0.8 shard_map.66
  66.5 48.9 %all_to_all.10 = bf16[256,5,2,128]{3,2,1,0:T(2,128)(2,1)S(1)} all-to-all(bf16[256,5,2,128]{3,2,1,0:T(2,128)(2,1)S(1)} %bitcast.34), channel_id=1, replica_groups={{276,308,340,372,404,436,468,500,20,52,84,116,148,180,212,244,284,316,3..., dimensions={0} | all-to-all | bytes 1310720 | tf_op jit(solution)/shard_map/all_to_all | solution.py:47
  115.4 0.6 fusion.5
  116.0 1.1 copy.34
  (31 shorter events, 1.4 us)
Async XLA Ops:
  0.0 30.4 %copy-start.4 = (s32[64]{0:T(128)S(1)}, s32[64]{0:T(128)}, u32[]{:S(2)}) copy-start(s32[64]{0:T(128)} %assignment.1) | copy-start | bytes 772
  0.0 33.0 %copy-start.2 = (s32[64,10,5]{0,2,1:T(8,128)S(1)}, s32[64,10,5]{0,2,1:T(8,128)}, u32[]{:S(2)}) copy-start(s32[64,10,5]{0,2,1:T(8,128)} %param.8) | copy-start | bytes 38404
  0.0 33.2 %copy-start.3 = (bf16[128,128]{1,0:T(8,128)(2,1)S(1)}, bf16[128,128]{1,0:T(8,128)(2,1)}, u32[]{:S(2)}) copy-start(bf16[128,128]{1,0:T(8,128)(2,1)} %param.11) | copy-start | bytes 98308
  3.5 56.1 %all-to-all-start = ((bf16[256,5,2,128]{3,2,1,0:T(2,128)(2,1)}), bf16[256,5,2,128]{3,2,1,0:T(2,128)(2,1)S(1)}, u32[]{:S(2)}, u32[]{:S(2)}) async-start(bf16[256,5,2,128]{3,2,1,0:T(2,128)(2,1)} %bitcast.38), calls=%async_computation | async-start | bytes 1310720 | tf_op jit(solution)/shard_map/all_to_all | solution.py:47
  37.4 1.4 %copy-start = (bf16[1,1280,640]{2,1,0:T(8,128)(2,1)S(1)}, bf16[1,1280,640]{2,1,0:T(8,128)(2,1)}, u32[]{:S(2)}) copy-start(bf16[1,1280,640]{2,1,0:T(8,128)(2,1)} %param.7) | copy-start | bytes 4915204
  61.7 4.0 %collective-permute-start = (bf16[640,512]{1,0:T(8,128)(2,1)S(1)}, bf16[640,512]{1,0:T(8,128)(2,1)S(1)}, u32[]{:S(2)}, u32[]{:S(2)}) collective-permute-start(bf16[640,512]{1,0:T(8,128)(2,1)S(1)} %shard_map.65.own), channel_id=1, source_target_pairs={{0,1},{1,0},{2,3},{3,2},{4,5},{5,4},{6,7},{7,6},{8,9},{9,8},{10,11... | collective-permute-start | bytes 1966088 | tf_op jit(solution)/shard_map/ppermute | solution.py:294
  63.8 51.6 %copy-start.1 = (bf16[1280,640]{1,0:T(8,128)(2,1)S(1)}, bf16[1280,640]{1,0:T(8,128)(2,1)}, u32[]{:S(2)}) copy-start(bf16[1280,640]{1,0:T(8,128)(2,1)} %bitcast_multiply_fusion) | copy-start | bytes 4915204

commit v6 on v5

--- a/solution.py
+++ b/solution.py
@@ -12,6 +12,7 @@
 F = 8
 TILE = 128
 LAT_CHUNKS = 2
+LAT_PARTS = 2
 PEERS = ("y", "x", "z")
 SIZES = {"z": 16, "x": 4, "y": 4, "core": 2}
 
@@ -116,13 +117,20 @@
             )
             tile = slice(TILE * t, TILE * (t + 1))
             matrix[tile, :] = matrix[tile, :] * keep
-        found = jnp.dot(
-            matrix[chunk * i : chunk * (i + 1), :],
-            coeffs[...],
-            preferred_element_type=jnp.float32,
-        )
-        for part in range(2):
-            wide[pl.ds(part, chunk, stride=2), :] = found[:, part * lanes : (part + 1) * lanes]
+        depth = chunk // LAT_PARTS
+        founds = [
+            jnp.dot(
+                matrix[pl.ds(chunk * i + depth * j, depth), :],
+                coeffs[...],
+                preferred_element_type=jnp.float32,
+            )
+            for j in range(LAT_PARTS)
+        ]
+        for j, found in enumerate(founds):
+            for part in range(2):
+                wide[pl.ds(2 * depth * j + part, depth, stride=2), :] = found[
+                    :, part * lanes : (part + 1) * lanes
+                ]
         merged[2 * chunk * i : 2 * chunk * (i + 1), :] = wide[...].astype(jnp.bfloat16)
         out_copy(i).start()
     for i in range(LAT_CHUNKS):
@@ -155,7 +163,7 @@
     )(spectral.reshape(2 * degrees, channels), legendre, pattern, assignment)
 
 
-def grid_kernel(lats, received, synthesis, analysis, returned, wide, ahead):
+def grid_kernel(lats, received, synthesis, analysis, returned, wide, ahead, back_rows, products):
     blocks, rows, lanes = received.shape
     width = blocks * lanes
     slots = rows // (2 * lats)
@@ -185,15 +193,16 @@
             jnp.dot(synthesis[...], gather(rows_of, lat), preferred_element_type=jnp.float32)
             for rows_of in (wide, ahead)
         )
-        product = (field * partner).astype(jnp.bfloat16)
-        back = jnp.dot(analysis[...], product, preferred_element_type=jnp.float32)
+        products[lat] = (field * partner).astype(jnp.bfloat16)
+    for lat in range(lats):
+        back = jnp.dot(analysis[...], products[lat], preferred_element_type=jnp.float32)
         for part in range(2):
             for i in range(blocks):
-                wide[i, span(lat, part), :] = back[
+                back_rows[i, span(lat, part), :] = back[
                     part * slots : (part + 1) * slots, i * lanes : (i + 1) * lanes
                 ]
     for i in range(blocks):
-        returned[:, i * lanes : (i + 1) * lanes] = wide[i].astype(jnp.bfloat16)
+        returned[:, i * lanes : (i + 1) * lanes] = back_rows[i].astype(jnp.bfloat16)
 
 
 def couple_kernel(own, other, own_matrix, other_matrix, weight, sent):
@@ -289,7 +298,8 @@
         received,
         synthesis,
         analysis,
-        scratch=[pltpu.VMEM((y_count, rows, channels), jnp.float32)] * 2,
+        scratch=[pltpu.VMEM((y_count, rows, channels), jnp.float32)] * 3
+        + [pltpu.VMEM((lats, lon_count, wide), jnp.bfloat16)],
     )
     swapped = lax.ppermute(returned, "core", [(0, 1), (1, 0)])
 

time: 117 us -> 116 us (level)
  no operation moved by 1% of the time
where the time goes in v6:
time: 116 us
  blocking collectives  48.9 us (42%)
  starting transfers between devices  28.8 us (25%)
  waiting for transfers between devices  21.2 us (18%)
  local copies, waits for them, and re-layouts  5.91 us (5%)
  Pallas kernels  5.09 us (4%)
  between operations  2.2 us (2%)
  other arithmetic  2.16 us (2%)
  matrix products  1.75 us (2%)
    all_to_all x1, blocking collectives, exchange(): lax.all_to_all(values, tuple(SIZES), split_axis=0, concat_axis=0, axis_in...  48.9 us
    all_to_all x1, starting transfers between devices, exchange(): lax.all_to_all(values, tuple(SIZES), split_axis=0, concat_axis=0, axis_in...  26.9 us
    all_to_all x1, waiting for transfers between devices, exchange(): lax.all_to_all(values, tuple(SIZES), split_axis=0, concat_axis=0, axis_in...  19.3 us
    pallas_call x1, Pallas kernels, forward(): pl.pallas_call(forward_kernel, out_shape=jax.ShapeDtypeStruct((2 * lat_co...  3 us
  transfers between devices with their start and end apart: 2, of which 2 were waited for; matrix products, arithmetic and copies ran while one was open for 6% of the time, Pallas kernels for 0%

profile of v6, /device:TPU:6, one launch (start us, length us, event | category | flops | bytes accessed | tf_op | source)
XLA Modules:
  0.0 116.0 jit_solution(7288627322431218900)
XLA Ops:
  0.0 3.0 %shard_map.64 = bf16[2560,128]{1,0:T(8,128)(2,1)} custom-call(bf16[1280,128]{1,0:T(8,128)(2,1)} %bitcast.40, bf16[1280,640]{1,0:T(8,128)(2,1)} %bitcast.37, s32[10,5,64]{2,1,0:T(8,128)} %bitcast.41, s32[64]{0:T(128)} %assignment.1), custom_call_target="tpu_custom_call" | custom-call | tf_op jit(solution)/shard_map/pallas_call | solution.py:145
  3.0 26.9 %all-to-all-start = ((bf16[256,5,2,128]{3,2,1,0:T(2,128)(2,1)}), bf16[256,5,2,128]{3,2,1,0:T(2,128)(2,1)S(1)}, u32[]{:S(2)}, u32[]{:S(2)}) async-start(bf16[256,5,2,128]{3,2,1,0:T(2,128)(2,1)} %bitcast.38), calls=%async_computation | async-start | bytes 1310720 | tf_op jit(solution)/shard_map/all_to_all | solution.py:48
  29.9 0.6 dynamic_slice.23
  32.5 0.1 copy.37
  32.7 0.1 slice.67
  33.1 0.8 dynamic_slice.22
  34.0 0.1 reshape.131
  34.2 0.2 fusion.31
  34.4 0.2 fusion.18
  35.4 0.4 fusion.24
  35.8 0.6 compare_select_fusion.other_matrix
  36.3 0.6 compare_select_fusion.1.own_matrix
  36.9 0.4 broadcast_in_dim.12
  37.3 1.0 copy-done
  38.3 1.5 %bitcast_multiply_fusion = bf16[1280,640]{1,0:T(8,128)(2,1)} fusion(bf16[160,8,5,128]{3,2,1,0:T(8,128)(2,1)S(1)} %bitcast.36, bf16[1,1280,640]{2,1,0:T(8,128)(2,1)S(1)} %copy-done), kind=kLoop, calls=%fused_computation | loop fusion | flops 819200 | bytes 4915200 | tf_op jit(solution)/shard_map/mul | solution.py:249
  39.8 19.3 %all-to-all-done = bf16[256,5,2,128]{3,2,1,0:T(2,128)(2,1)S(1)} async-done(((bf16[256,5,2,128]{3,2,1,0:T(2,128)(2,1)}), bf16[256,5,2,128]{3,2,1,0:T(2,128)(2,1)S(1)}, u32[]{:S(2)}, u32[]{:S(2)}) %all-to-all-start) | async-done | bytes 655392 | tf_op jit(solution)/shard_map/all_to_all | solution.py:48
  59.3 1.3 %shard_map.65.own = bf16[640,512]{1,0:T(8,128)(2,1)S(1)} custom-call(bf16[4,640,128]{2,1,0:T(8,128)(2,1)S(1)} %bitcast.35, bf16[192,128]{1,0:T(8,128)(2,1)S(1)} %copy.30.synthesis, bf16[128,192]{1,0:T(8,128)(2,1)S(1)} %get-tuple-element.15.analysis), custom_call_target="tpu_custom_call" | custom-call | flops 251658240 | bytes 1409024 | tf_op jit(solution)/shard_map/pallas_call | solution.py:219
  60.5 1.9 %collective-permute-start = (bf16[640,512]{1,0:T(8,128)(2,1)S(1)}, bf16[640,512]{1,0:T(8,128)(2,1)S(1)}, u32[]{:S(2)}, u32[]{:S(2)}) collective-permute-start(bf16[640,512]{1,0:T(8,128)(2,1)S(1)} %shard_map.65.own), channel_id=1, source_target_pairs={{0,1},{1,0},{2,3},{3,2},{4,5},{5,4},{6,7},{7,6},{8,9},{9,8},{10,11... | collective-permute-start | bytes 1966088 | tf_op jit(solution)/shard_map/ppermute | solution.py:304
  62.5 0.2 copy.31.weight
  62.6 1.9 %collective-permute-done.other = bf16[640,512]{1,0:T(8,128)(2,1)S(1)} collective-permute-done((bf16[640,512]{1,0:T(8,128)(2,1)S(1)}, bf16[640,512]{1,0:T(8,128)(2,1)S(1)}, u32[]{:S(2)}, u32[]{:S(2)}) %collective-permute-start) | collective-permute-done | bytes 655392 | tf_op jit(solution)/shard_map/ppermute | solution.py:304
  64.5 0.8 shard_map.66
  65.4 48.9 %all_to_all.10 = bf16[256,5,2,128]{3,2,1,0:T(2,128)(2,1)S(1)} all-to-all(bf16[256,5,2,128]{3,2,1,0:T(2,128)(2,1)S(1)} %bitcast.34), channel_id=1, replica_groups={{276,308,340,372,404,436,468,500,20,52,84,116,148,180,212,244,284,316,3..., dimensions={0} | all-to-all | bytes 1310720 | tf_op jit(solution)/shard_map/all_to_all | solution.py:48
  114.2 0.6 fusion.5
  114.9 1.1 copy.34
  (31 shorter events, 1.4 us)
Async XLA Ops:
  0.0 29.9 %copy-start.4 = (s32[64]{0:T(128)S(1)}, s32[64]{0:T(128)}, u32[]{:S(2)}) copy-start(s32[64]{0:T(128)} %assignment.1) | copy-start | bytes 772
  0.0 32.4 %copy-start.2 = (s32[64,10,5]{0,2,1:T(8,128)S(1)}, s32[64,10,5]{0,2,1:T(8,128)}, u32[]{:S(2)}) copy-start(s32[64,10,5]{0,2,1:T(8,128)} %param.8) | copy-start | bytes 38404
  0.0 32.7 %copy-start.3 = (bf16[128,128]{1,0:T(8,128)(2,1)S(1)}, bf16[128,128]{1,0:T(8,128)(2,1)}, u32[]{:S(2)}) copy-start(bf16[128,128]{1,0:T(8,128)(2,1)} %param.11) | copy-start | bytes 98308
  3.0 56.1 %all-to-all-start = ((bf16[256,5,2,128]{3,2,1,0:T(2,128)(2,1)}), bf16[256,5,2,128]{3,2,1,0:T(2,128)(2,1)S(1)}, u32[]{:S(2)}, u32[]{:S(2)}) async-start(bf16[256,5,2,128]{3,2,1,0:T(2,128)(2,1)} %bitcast.38), calls=%async_computation | async-start | bytes 1310720 | tf_op jit(solution)/shard_map/all_to_all | solution.py:48
  36.9 1.4 %copy-start = (bf16[1,1280,640]{2,1,0:T(8,128)(2,1)S(1)}, bf16[1,1280,640]{2,1,0:T(8,128)(2,1)}, u32[]{:S(2)}) copy-start(bf16[1,1280,640]{2,1,0:T(8,128)(2,1)} %param.7) | copy-start | bytes 4915204
  60.5 4.0 %collective-permute-start = (bf16[640,512]{1,0:T(8,128)(2,1)S(1)}, bf16[640,512]{1,0:T(8,128)(2,1)S(1)}, u32[]{:S(2)}, u32[]{:S(2)}) collective-permute-start(bf16[640,512]{1,0:T(8,128)(2,1)S(1)} %shard_map.65.own), channel_id=1, source_target_pairs={{0,1},{1,0},{2,3},{3,2},{4,5},{5,4},{6,7},{7,6},{8,9},{9,8},{10,11... | collective-permute-start | bytes 1966088 | tf_op jit(solution)/shard_map/ppermute | solution.py:304
  62.6 51.6 %copy-start.1 = (bf16[1280,640]{1,0:T(8,128)(2,1)S(1)}, bf16[1280,640]{1,0:T(8,128)(2,1)}, u32[]{:S(2)}) copy-start(bf16[1280,640]{1,0:T(8,128)(2,1)} %bitcast_multiply_fusion) | copy-start | bytes 4915204

commit v7 on v6

--- a/solution.py
+++ b/solution.py
@@ -205,9 +205,12 @@
         returned[:, i * lanes : (i + 1) * lanes] = back_rows[i].astype(jnp.bfloat16)
 
 
-def couple_kernel(own, other, own_matrix, other_matrix, weight, sent):
-    total = jnp.dot(own[...], own_matrix[...], preferred_element_type=jnp.float32)
-    total += jnp.dot(other[...], other_matrix[...], preferred_element_type=jnp.float32)
+def own_kernel(own, own_matrix, total):
+    total[...] = jnp.dot(own[...], own_matrix[...], preferred_element_type=jnp.float32)
+
+
+def couple_kernel(begun, other, other_matrix, weight, sent):
+    total = begun[...] + jnp.dot(other[...], other_matrix[...], preferred_element_type=jnp.float32)
     total *= weight[...]
     blocks, rows, lanes = sent.shape
     for i in range(blocks):
@@ -303,14 +306,21 @@
     )
     swapped = lax.ppermute(returned, "core", [(0, 1), (1, 0)])
 
+    begun = call(
+        own_kernel,
+        jax.ShapeDtypeStruct((rows, wide), jnp.float32),
+        2 * rows * wide * wide,
+        16,
+        returned,
+        own_matrix,
+    )
     sent = call(
         couple_kernel,
         jax.ShapeDtypeStruct((y_count, rows, channels), jnp.bfloat16),
-        4 * rows * wide * wide,
+        2 * rows * wide * wide,
         16,
-        returned,
+        begun,
         swapped,
-        own_matrix,
         other_matrix,
         weight,
     )

time: 116 us -> 116 us (level)
  no operation moved by 1% of the time
where the time goes in v7:
time: 116 us
  blocking collectives  48.9 us (42%)
  starting transfers between devices  28.8 us (25%)
  waiting for transfers between devices  20.7 us (18%)
  local copies, waits for them, and re-layouts  5.91 us (5%)
  Pallas kernels  5.26 us (5%)
  between operations  2.2 us (2%)
  other arithmetic  2.16 us (2%)
  matrix products  1.75 us (2%)
    all_to_all x1, blocking collectives, exchange(): lax.all_to_all(values, tuple(SIZES), split_axis=0, concat_axis=0, axis_in...  48.9 us
    all_to_all x1, starting transfers between devices, exchange(): lax.all_to_all(values, tuple(SIZES), split_axis=0, concat_axis=0, axis_in...  26.9 us
    all_to_all x1, waiting for transfers between devices, exchange(): lax.all_to_all(values, tuple(SIZES), split_axis=0, concat_axis=0, axis_in...  19.3 us
    pallas_call x1, Pallas kernels, forward(): pl.pallas_call(forward_kernel, out_shape=jax.ShapeDtypeStruct((2 * lat_co...  3 us
  transfers between devices with their start and end apart: 2, of which 2 were waited for; matrix products, arithmetic and copies ran while one was open for 6% of the time, Pallas kernels for 0%

profile of v7, /device:TPU:6, one launch (start us, length us, event | category | flops | bytes accessed | tf_op | source)
XLA Modules:
  0.0 115.6 jit_solution(5526877975652010854)
XLA Ops:
  0.0 3.0 %shard_map.64 = bf16[2560,128]{1,0:T(8,128)(2,1)} custom-call(bf16[1280,128]{1,0:T(8,128)(2,1)} %bitcast.40, bf16[1280,640]{1,0:T(8,128)(2,1)} %bitcast.37, s32[10,5,64]{2,1,0:T(8,128)} %bitcast.41, s32[64]{0:T(128)} %assignment.1), custom_call_target="tpu_custom_call" | custom-call | tf_op jit(solution)/shard_map/pallas_call | solution.py:145
  3.0 26.9 %all-to-all-start = ((bf16[256,5,2,128]{3,2,1,0:T(2,128)(2,1)}), bf16[256,5,2,128]{3,2,1,0:T(2,128)(2,1)S(1)}, u32[]{:S(2)}, u32[]{:S(2)}) async-start(bf16[256,5,2,128]{3,2,1,0:T(2,128)(2,1)} %bitcast.38), calls=%async_computation | async-start | bytes 1310720 | tf_op jit(solution)/shard_map/all_to_all | solution.py:48
  29.9 0.6 dynamic_slice.23
  32.7 0.1 slice.67
  33.1 0.8 dynamic_slice.22
  34.0 0.1 reshape.131
  34.2 0.2 fusion.31
  34.4 0.2 fusion.18
  35.4 0.4 fusion.24
  35.8 0.6 compare_select_fusion.other_matrix
  36.3 0.6 compare_select_fusion.1.own_matrix
  36.9 0.4 broadcast_in_dim.12
  37.3 1.0 copy-done
  38.3 1.5 %bitcast_multiply_fusion = bf16[1280,640]{1,0:T(8,128)(2,1)} fusion(bf16[160,8,5,128]{3,2,1,0:T(8,128)(2,1)S(1)} %bitcast.36, bf16[1,1280,640]{2,1,0:T(8,128)(2,1)S(1)} %copy-done), kind=kLoop, calls=%fused_computation | loop fusion | flops 819200 | bytes 4915200 | tf_op jit(solution)/shard_map/mul | solution.py:252
  39.8 19.3 %all-to-all-done = bf16[256,5,2,128]{3,2,1,0:T(2,128)(2,1)S(1)} async-done(((bf16[256,5,2,128]{3,2,1,0:T(2,128)(2,1)}), bf16[256,5,2,128]{3,2,1,0:T(2,128)(2,1)S(1)}, u32[]{:S(2)}, u32[]{:S(2)}) %all-to-all-start) | async-done | bytes 655392 | tf_op jit(solution)/shard_map/all_to_all | solution.py:48
  59.3 1.3 %shard_map.65.own = bf16[640,512]{1,0:T(8,128)(2,1)S(1)} custom-call(bf16[4,640,128]{2,1,0:T(8,128)(2,1)S(1)} %bitcast.34, bf16[192,128]{1,0:T(8,128)(2,1)S(1)} %copy.30.synthesis, bf16[128,192]{1,0:T(8,128)(2,1)S(1)} %get-tuple-element.15.analysis), custom_call_target="tpu_custom_call" | custom-call | flops 251658240 | bytes 1409024 | tf_op jit(solution)/shard_map/pallas_call | solution.py:222
  60.5 1.9 %collective-permute-start = (bf16[640,512]{1,0:T(8,128)(2,1)S(1)}, bf16[640,512]{1,0:T(8,128)(2,1)S(1)}, u32[]{:S(2)}, u32[]{:S(2)}) collective-permute-start(bf16[640,512]{1,0:T(8,128)(2,1)S(1)} %shard_map.65.own), channel_id=1, source_target_pairs={{0,1},{1,0},{2,3},{3,2},{4,5},{5,4},{6,7},{7,6},{8,9},{9,8},{10,11... | collective-permute-start | bytes 1966088 | tf_op jit(solution)/shard_map/ppermute | solution.py:307
  62.5 0.2 copy.31.weight
  62.6 0.5 shard_map.66.begun
  63.2 1.4 %collective-permute-done.other = bf16[640,512]{1,0:T(8,128)(2,1)S(1)} collective-permute-done((bf16[640,512]{1,0:T(8,128)(2,1)S(1)}, bf16[640,512]{1,0:T(8,128)(2,1)S(1)}, u32[]{:S(2)}, u32[]{:S(2)}) %collective-permute-start) | collective-permute-done | bytes 655392 | tf_op jit(solution)/shard_map/ppermute | solution.py:307
  64.5 0.5 shard_map.67
  65.0 48.9 %all_to_all.10 = bf16[256,5,2,128]{3,2,1,0:T(2,128)(2,1)S(1)} all-to-all(bf16[256,5,2,128]{3,2,1,0:T(2,128)(2,1)S(1)} %bitcast.35), channel_id=1, replica_groups={{276,308,340,372,404,436,468,500,20,52,84,116,148,180,212,244,284,316,3..., dimensions={0} | all-to-all | bytes 1310720 | tf_op jit(solution)/shard_map/all_to_all | solution.py:48
  113.9 0.6 fusion.5
  114.6 1.1 copy.34
  (32 shorter events, 1.5 us)
Async XLA Ops:
  0.0 29.9 %copy-start.4 = (s32[64]{0:T(128)S(1)}, s32[64]{0:T(128)}, u32[]{:S(2)}) copy-start(s32[64]{0:T(128)} %assignment.1) | copy-start | bytes 772
  0.0 32.4 %copy-start.2 = (s32[64,10,5]{0,2,1:T(8,128)S(1)}, s32[64,10,5]{0,2,1:T(8,128)}, u32[]{:S(2)}) copy-start(s32[64,10,5]{0,2,1:T(8,128)} %param.8) | copy-start | bytes 38404
  0.0 32.7 %copy-start.3 = (bf16[128,128]{1,0:T(8,128)(2,1)S(1)}, bf16[128,128]{1,0:T(8,128)(2,1)}, u32[]{:S(2)}) copy-start(bf16[128,128]{1,0:T(8,128)(2,1)} %param.11) | copy-start | bytes 98308
  3.0 56.1 %all-to-all-start = ((bf16[256,5,2,128]{3,2,1,0:T(2,128)(2,1)}), bf16[256,5,2,128]{3,2,1,0:T(2,128)(2,1)S(1)}, u32[]{:S(2)}, u32[]{:S(2)}) async-start(bf16[256,5,2,128]{3,2,1,0:T(2,128)(2,1)} %bitcast.38), calls=%async_computation | async-start | bytes 1310720 | tf_op jit(solution)/shard_map/all_to_all | solution.py:48
  36.9 1.4 %copy-start = (bf16[1,1280,640]{2,1,0:T(8,128)(2,1)S(1)}, bf16[1,1280,640]{2,1,0:T(8,128)(2,1)}, u32[]{:S(2)}) copy-start(bf16[1,1280,640]{2,1,0:T(8,128)(2,1)} %param.7) | copy-start | bytes 4915204
  60.5 4.0 %collective-permute-start = (bf16[640,512]{1,0:T(8,128)(2,1)S(1)}, bf16[640,512]{1,0:T(8,128)(2,1)S(1)}, u32[]{:S(2)}, u32[]{:S(2)}) collective-permute-start(bf16[640,512]{1,0:T(8,128)(2,1)S(1)} %shard_map.65.own), channel_id=1, source_target_pairs={{0,1},{1,0},{2,3},{3,2},{4,5},{5,4},{6,7},{7,6},{8,9},{9,8},{10,11... | collective-permute-start | bytes 1966088 | tf_op jit(solution)/shard_map/ppermute | solution.py:307
  63.1 50.8 %copy-start.1 = (bf16[1280,640]{1,0:T(8,128)(2,1)S(1)}, bf16[1280,640]{1,0:T(8,128)(2,1)}, u32[]{:S(2)}) copy-start(bf16[1280,640]{1,0:T(8,128)(2,1)} %bitcast_multiply_fusion) | copy-start | bytes 4915204

commit v8 on v7

--- a/solution.py
+++ b/solution.py
@@ -217,6 +217,57 @@
         sent[i] = total[:, i * lanes : (i + 1) * lanes].astype(jnp.bfloat16)
 
 
+def backward_kernel(weighted, pruned_t, result, paired, coeffs, wide, merged, out_sem):
+    degrees, lat_count = pruned_t.shape
+    lanes = weighted.shape[1]
+    paired[...] = weighted[...].astype(jnp.float32)
+    for part in range(2):
+        coeffs[:, part * lanes : (part + 1) * lanes] = paired[
+            pl.ds(part, lat_count, stride=2), :
+        ].astype(jnp.bfloat16)
+    depth = degrees // 2
+    founds = [
+        jnp.dot(
+            pruned_t[depth * j : depth * (j + 1), :],
+            coeffs[...],
+            preferred_element_type=jnp.float32,
+        )
+        for j in range(2)
+    ]
+    copies = []
+    for j, found in enumerate(founds):
+        for part in range(2):
+            wide[pl.ds(2 * depth * j + part, depth, stride=2), :] = found[
+                :, part * lanes : (part + 1) * lanes
+            ]
+        span = pl.ds(2 * depth * j, 2 * depth)
+        merged[span, :] = wide[span, :].astype(jnp.bfloat16)
+        copy = pltpu.make_async_copy(merged.at[span], result.at[span], out_sem.at[j])
+        copy.start()
+        copies.append(copy)
+    for copy in copies:
+        copy.wait()
+
+
+def backward(weighted, pruned_t):
+    degrees, lat_count = pruned_t.shape
+    channels = weighted.shape[1]
+    return pl.pallas_call(
+        backward_kernel,
+        out_shape=jax.ShapeDtypeStruct((2 * degrees, channels), jnp.bfloat16),
+        in_specs=[pl.BlockSpec(memory_space=pltpu.VMEM)] * 2,
+        out_specs=pl.BlockSpec(memory_space=pltpu.HBM),
+        scratch_shapes=[
+            pltpu.VMEM((2 * lat_count, channels), jnp.float32),
+            pltpu.VMEM((lat_count, 2 * channels), jnp.bfloat16),
+            pltpu.VMEM((2 * degrees, channels), jnp.float32),
+            pltpu.VMEM((2 * degrees, channels), jnp.bfloat16),
+            pltpu.SemaphoreType.DMA((2,)),
+        ],
+        compiler_params=pltpu.CompilerParams(vmem_limit_bytes=16 << 20),
+    )(weighted, pruned_t)
+
+
 def call(kernel, out_shape, flops, limit, *operands, scratch=()):
     moved = sum(x.size * x.dtype.itemsize for x in operands) + out_shape.size * 2
     return pl.pallas_call(
@@ -245,12 +296,6 @@
 
     own_wave = lax.dynamic_index_in_dim(assignment, slot, 0, keepdims=False)
     own_mask = lax.dynamic_index_in_dim(pattern, own_wave, 0, keepdims=False).astype(jnp.bfloat16)
-    lat_tiles, deg_tiles = own_mask.shape
-    wide_mask = jnp.broadcast_to(
-        own_mask[:, None, :, None], (lat_tiles, TILE, deg_tiles, TILE)
-    ).reshape(lat_count, degrees)
-    pruned = legendre[0] * wide_mask
-
     at_lats = forward(spectral[0], legendre[0], pattern, assignment)
     at_lats = at_lats.reshape(peers, lats, 2, channels)
     received = exchange(at_lats)
@@ -285,9 +330,9 @@
     weight = lax.dynamic_slice_in_dim(quad_weight, group * lats, lats)
     weight = jnp.broadcast_to(weight[None, :, None], (wave_total, lats, 2)).reshape(rows, 1)
     own_matrix, other_matrix = matrix(core), matrix(1 - core)
-    received, synthesis, analysis, own_matrix, other_matrix, weight, pruned = (
+    received, synthesis, analysis, own_matrix, other_matrix, weight, own_mask = (
         lax.optimization_barrier(
-            (received, synthesis, analysis, own_matrix, other_matrix, weight, pruned)
+            (received, synthesis, analysis, own_matrix, other_matrix, weight, own_mask)
         )
     )
 
@@ -324,11 +369,16 @@
         other_matrix,
         weight,
     )
+    sent, own_mask = lax.optimization_barrier((sent, own_mask))
+    lat_tiles, deg_tiles = own_mask.shape
+    wide_mask = jnp.broadcast_to(
+        own_mask[:, None, :, None], (lat_tiles, TILE, deg_tiles, TILE)
+    ).reshape(lat_count, degrees)
+    pruned_t = (legendre[0] * wide_mask).T
     sent = sent.reshape(peers, lats, 2, channels)
     weighted = exchange(sent)
-    weighted = weighted.reshape(lat_count, 2, channels)
-    tendency = jnp.einsum("ln,lch->nch", pruned, weighted, preferred_element_type=jnp.float32)
-    return tendency.astype(jnp.bfloat16)[None]
+    tendency = backward(weighted.reshape(2 * lat_count, channels), pruned_t)
+    return tendency.reshape(1, degrees, 2, channels)
 
 
 def solution(mesh):

time: 116 us -> 117 us (level)
  blocking collectives: 48.9 us -> 0 us
  waiting for transfers between devices: 20.7 us -> 44.5 us
  starting transfers between devices: 28.8 us -> 48.3 us
  local copies, waits for them, and re-layouts: 5.91 us -> 9.94 us
  Pallas kernels: 5.26 us -> 7.6 us
    all_to_all x1 -> x0, blocking collectives: 48.9 us -> none  [exchange(): lax.all_to_all(values, tuple(SIZES), split_axis=0, concat_axis=0, axis_in...]
    all_to_all x1 -> x2, waiting for transfers between devices: 19.3 us -> 43.2 us  [exchange(): lax.all_to_all(values, tuple(SIZES), split_axis=0, concat_axis=0, axis_in...]
    all_to_all x1 -> x2, starting transfers between devices: 26.9 us -> 46.4 us  [exchange(): lax.all_to_all(values, tuple(SIZES), split_axis=0, concat_axis=0, axis_in...]
    unnamed x12 -> x10, local copies, waits for them, and re-layouts: 1.2 us -> 4.1 us
    reshape x0 -> x1, local copies, waits for them, and re-layouts: none -> 2.2 us  [local(): wide_mask = jnp.broadcast_to(own_mask[:, None, :, None], (lat_tiles, TILE...]
    transpose x0 -> x1, other arithmetic: none -> 2.09 us  [local(): pruned_t = (legendre[0] * wide_mask).T]
    mul x1 -> x0, other arithmetic: 1.5 us -> none  [local(): pruned = legendre[0] * wide_mask]
    pallas_call x0 -> x1, Pallas kernels: none -> 1.48 us  [backward(): pl.pallas_call(backward_kernel, out_shape=jax.ShapeDtypeStruct((2 * degre...]
  transfers between devices with their start and end apart: 2 -> 3, of which waited for: 2 -> 3; matrix products, arithmetic and copies ran while one was open for 6% -> 12% of each run, Pallas kernels for 0% -> 0%
where the time goes in v8:
time: 117 us
  starting transfers between devices  48.3 us (41%)
  waiting for transfers between devices  44.5 us (38%)
  local copies, waits for them, and re-layouts  9.94 us (8%)
  Pallas kernels  7.6 us (6%)
  other arithmetic  2.75 us (2%)
  between operations  2.36 us (2%)
    all_to_all x2, starting transfers between devices, exchange(): lax.all_to_all(values, tuple(SIZES), split_axis=0, concat_axis=0, axis_in...  46.4 us
    all_to_all x2, waiting for transfers between devices, exchange(): lax.all_to_all(values, tuple(SIZES), split_axis=0, concat_axis=0, axis_in...  43.2 us
    unnamed x10, local copies, waits for them, and re-layouts  4.1 us
    pallas_call x3, Pallas kernels, call(): pl.pallas_call(kernel, out_shape=out_shape, in_specs=[pl.BlockSpec(memory...  3.12 us
    pallas_call x1, Pallas kernels, forward(): pl.pallas_call(forward_kernel, out_shape=jax.ShapeDtypeStruct((2 * lat_co...  3 us
  transfers between devices with their start and end apart: 3, of which 3 were waited for; matrix products, arithmetic and copies ran while one was open for 12% of the time, Pallas kernels for 0%

profile of v8, /device:TPU:6, one launch (start us, length us, event | category | flops | bytes accessed | tf_op | source)
XLA Modules:
  0.0 116.6 jit_solution(2029293780034438709)
XLA Ops:
  0.0 3.0 %shard_map.64 = bf16[2560,128]{1,0:T(8,128)(2,1)} custom-call(bf16[1280,128]{1,0:T(8,128)(2,1)} %bitcast.38, bf16[1280,640]{1,0:T(8,128)(2,1)} %bitcast.35, s32[10,5,64]{2,1,0:T(8,128)} %bitcast.39, s32[64]{0:T(128)} %assignment.1), custom_call_target="tpu_custom_call" | custom-call | tf_op jit(solution)/shard_map/pallas_call | solution.py:145
  3.0 26.9 %all-to-all-start = ((bf16[256,5,2,128]{3,2,1,0:T(2,128)(2,1)}), bf16[256,5,2,128]{3,2,1,0:T(2,128)(2,1)S(1)}, u32[]{:S(2)}, u32[]{:S(2)}) async-start(bf16[256,5,2,128]{3,2,1,0:T(2,128)(2,1)} %bitcast.37), calls=%async_computation | async-start | bytes 1310720 | tf_op jit(solution)/shard_map/all_to_all | solution.py:48
  30.0 0.6 dynamic_slice.23
  32.8 0.2 fusion.23
  33.0 0.2 fusion.10
  33.4 0.8 dynamic_slice.22
  35.3 0.4 fusion.16
  35.7 0.6 compare_select_fusion.1.own_matrix
  36.2 0.6 compare_select_fusion.other_matrix
  36.8 22.3 %all-to-all-done = bf16[256,5,2,128]{3,2,1,0:T(2,128)(2,1)S(1)} async-done(((bf16[256,5,2,128]{3,2,1,0:T(2,128)(2,1)}), bf16[256,5,2,128]{3,2,1,0:T(2,128)(2,1)S(1)}, u32[]{:S(2)}, u32[]{:S(2)}) %all-to-all-start) | async-done | bytes 655392 | tf_op jit(solution)/shard_map/all_to_all | solution.py:48
  59.3 1.2 %shard_map.65.own = bf16[640,512]{1,0:T(8,128)(2,1)S(1)} custom-call(bf16[4,640,128]{2,1,0:T(8,128)(2,1)S(1)} %bitcast.33, bf16[192,128]{1,0:T(8,128)(2,1)S(1)} %copy.29.synthesis, bf16[128,192]{1,0:T(8,128)(2,1)S(1)} %get-tuple-element.16.analysis), custom_call_target="tpu_custom_call" | custom-call | flops 251658240 | bytes 1409024 | tf_op jit(solution)/shard_map/pallas_call | solution.py:273
  60.5 1.9 %collective-permute-start = (bf16[640,512]{1,0:T(8,128)(2,1)S(1)}, bf16[640,512]{1,0:T(8,128)(2,1)S(1)}, u32[]{:S(2)}, u32[]{:S(2)}) collective-permute-start(bf16[640,512]{1,0:T(8,128)(2,1)S(1)} %shard_map.65.own), channel_id=1, source_target_pairs={{0,1},{1,0},{2,3},{3,2},{4,5},{5,4},{6,7},{7,6},{8,9},{9,8},{10,11... | collective-permute-start | bytes 1966088 | tf_op jit(solution)/shard_map/ppermute | solution.py:352
  62.4 0.2 copy.30.weight
  62.6 0.5 shard_map.66.begun
  63.1 1.4 %collective-permute-done.other = bf16[640,512]{1,0:T(8,128)(2,1)S(1)} collective-permute-done((bf16[640,512]{1,0:T(8,128)(2,1)S(1)}, bf16[640,512]{1,0:T(8,128)(2,1)S(1)}, u32[]{:S(2)}, u32[]{:S(2)}) %collective-permute-start) | collective-permute-done | bytes 655392 | tf_op jit(solution)/shard_map/ppermute | solution.py:352
  64.5 1.4 %shard_map.67 = bf16[4,640,128]{2,1,0:T(8,128)(2,1)} custom-call(f32[640,512]{1,0:T(8,128)S(1)} %shard_map.66.begun, bf16[640,512]{1,0:T(8,128)(2,1)S(1)} %collective-permute-done.other, bf16[512,512]{1,0:T(8,128)(2,1)S(1)} %compare_select_fusion.other_matrix, f32[640,1]{1,0:T(8,128)S(1)} %copy.30.weight), custom_call_target="tpu_custom_call" | custom-call | flops 335544320 | bytes 3148288 | tf_op jit(solution)/shard_map/pallas_call | solution.py:273
  65.9 19.5 %all-to-all-start.1 = ((bf16[256,5,2,128]{3,2,1,0:T(2,128)(2,1)}), bf16[256,5,2,128]{3,2,1,0:T(2,128)(2,1)S(1)}, u32[]{:S(2)}, u32[]{:S(2)}) async-start(bf16[256,5,2,128]{3,2,1,0:T(2,128)(2,1)} %bitcast.10), calls=%async_computation.1 | async-start | bytes 1310720 | tf_op jit(solution)/shard_map/all_to_all | solution.py:48
  85.4 3.5 %copy.22 = bf16[1,1280,640]{1,2,0:T(8,128)(2,1)} copy(bf16[1,1280,640]{2,1,0:T(8,128)(2,1)} %param.7) | data formatting | bytes 3276800 | tf_op args[1]
  89.0 0.4 broadcast_in_dim.11
  89.5 0.4 copy.39
  89.8 2.2 %copy.32 = bf16[1280,640]{0,1:T(8,128)(2,1)} copy(bf16[1280,640]{1,0:T(8,128)(2,1)S(1)} %bitcast.36) | data formatting | bytes 3276800 | tf_op jit(solution)/shard_map/reshape | solution.py:376
  92.0 2.1 %fusion.pruned_t = bf16[640,1280]{1,0:T(8,128)(2,1)S(1)} fusion(bf16[1280,640]{0,1:T(8,128)(2,1)} %copy.32, bf16[1,1280,640]{1,2,0:T(8,128)(2,1)} %copy.22), kind=kLoop, calls=%fused_computation.2 | loop fusion | flops 819200 | bytes 4915200 | tf_op jit(solution)/shard_map/transpose | solution.py:377
  94.1 20.8 %all-to-all-done.1 = bf16[256,5,2,128]{3,2,1,0:T(2,128)(2,1)S(1)} async-done(((bf16[256,5,2,128]{3,2,1,0:T(2,128)(2,1)}), bf16[256,5,2,128]{3,2,1,0:T(2,128)(2,1)S(1)}, u32[]{:S(2)}, u32[]{:S(2)}) %all-to-all-start.1) | async-done | bytes 655392 | tf_op jit(solution)/shard_map/all_to_all | solution.py:48
  115.0 1.5 %shard_map.68 = bf16[1280,128]{1,0:T(8,128)(2,1)} custom-call(bf16[2560,128]{1,0:T(8,128)(2,1)S(1)} %bitcast.32, bf16[640,1280]{1,0:T(8,128)(2,1)S(1)} %fusion.pruned_t), custom_call_target="tpu_custom_call" | custom-call | tf_op jit(solution)/shard_map/pallas_call | solution.py:255
  (31 shorter events, 1.8 us)
Async XLA Ops:
  0.0 29.9 %copy-start.2 = (s32[64]{0:T(128)S(1)}, s32[64]{0:T(128)}, u32[]{:S(2)}) copy-start(s32[64]{0:T(128)} %assignment.1) | copy-start | bytes 772
  0.0 32.4 %copy-start.1 = (bf16[128,128]{1,0:T(8,128)(2,1)S(1)}, bf16[128,128]{1,0:T(8,128)(2,1)}, u32[]{:S(2)}) copy-start(bf16[128,128]{1,0:T(8,128)(2,1)} %param.11) | copy-start | bytes 98308
  3.0 56.1 %all-to-all-start = ((bf16[256,5,2,128]{3,2,1,0:T(2,128)(2,1)}), bf16[256,5,2,128]{3,2,1,0:T(2,128)(2,1)S(1)}, u32[]{:S(2)}, u32[]{:S(2)}) async-start(bf16[256,5,2,128]{3,2,1,0:T(2,128)(2,1)} %bitcast.37), calls=%async_computation | async-start | bytes 1310720 | tf_op jit(solution)/shard_map/all_to_all | solution.py:48
  29.9 5.2 %copy-start = (s32[64,10,5]{0,2,1:T(8,128)S(1)}, s32[64,10,5]{0,2,1:T(8,128)}, u32[]{:S(2)}) copy-start(s32[64,10,5]{0,2,1:T(8,128)} %param.8) | copy-start | bytes 38404
  60.5 4.0 %collective-permute-start = (bf16[640,512]{1,0:T(8,128)(2,1)S(1)}, bf16[640,512]{1,0:T(8,128)(2,1)S(1)}, u32[]{:S(2)}, u32[]{:S(2)}) collective-permute-start(bf16[640,512]{1,0:T(8,128)(2,1)S(1)} %shard_map.65.own), channel_id=1, source_target_pairs={{0,1},{1,0},{2,3},{3,2},{4,5},{5,4},{6,7},{7,6},{8,9},{9,8},{10,11... | collective-permute-start | bytes 1966088 | tf_op jit(solution)/shard_map/ppermute | solution.py:352
  65.9 49.1 %all-to-all-start.1 = ((bf16[256,5,2,128]{3,2,1,0:T(2,128)(2,1)}), bf16[256,5,2,128]{3,2,1,0:T(2,128)(2,1)S(1)}, u32[]{:S(2)}, u32[]{:S(2)}) async-start(bf16[256,5,2,128]{3,2,1,0:T(2,128)(2,1)} %bitcast.10), calls=%async_computation.1 | async-start | bytes 1310720 | tf_op jit(solution)/shard_map/all_to_all | solution.py:48

commit v9 on v8

--- a/solution.py
+++ b/solution.py
@@ -163,7 +163,9 @@
     )(spectral.reshape(2 * degrees, channels), legendre, pattern, assignment)
 
 
-def grid_kernel(lats, received, synthesis, analysis, returned, wide, ahead, back_rows, products):
+def grid_kernel(
+    lats, received, synthesis, analysis, weight, returned, wide, ahead, back_rows, products
+):
     blocks, rows, lanes = received.shape
     width = blocks * lanes
     slots = rows // (2 * lats)
@@ -196,6 +198,7 @@
         products[lat] = (field * partner).astype(jnp.bfloat16)
     for lat in range(lats):
         back = jnp.dot(analysis[...], products[lat], preferred_element_type=jnp.float32)
+        back = back * weight[lat : lat + 1, :]
         for part in range(2):
             for i in range(blocks):
                 back_rows[i, span(lat, part), :] = back[
@@ -205,13 +208,30 @@
         returned[:, i * lanes : (i + 1) * lanes] = back_rows[i].astype(jnp.bfloat16)
 
 
-def own_kernel(own, own_matrix, total):
-    total[...] = jnp.dot(own[...], own_matrix[...], preferred_element_type=jnp.float32)
-
-
-def couple_kernel(begun, other, other_matrix, weight, sent):
+def level_matrix(small, width):
+    levels = small.shape[0]
+    channel = lax.broadcasted_iota(jnp.int32, (width, levels), 0) // F
+    level = lax.broadcasted_iota(jnp.int32, (width, levels), 1)
+    spread = (channel == level).astype(jnp.bfloat16)
+    contract = (((1,), (1,)), ((), ()))
+    tall = lax.dot_general(spread, small, contract, preferred_element_type=jnp.float32)
+    tall = tall.astype(jnp.bfloat16)
+    full = lax.dot_general(tall, spread, contract, preferred_element_type=jnp.float32)
+    source = lax.broadcasted_iota(jnp.int32, (width, width), 0) % F
+    target = lax.broadcasted_iota(jnp.int32, (width, width), 1) % F
+    return jnp.where(source == target, full, 0.0).astype(jnp.bfloat16)
+
+
+def own_kernel(own, own_small, other_small, total, other_matrix):
+    width = own.shape[1]
+    total[...] = jnp.dot(
+        own[...], level_matrix(own_small[...], width), preferred_element_type=jnp.float32
+    )
+    other_matrix[...] = level_matrix(other_small[...], width)
+
+
+def couple_kernel(begun, other, other_matrix, sent):
     total = begun[...] + jnp.dot(other[...], other_matrix[...], preferred_element_type=jnp.float32)
-    total *= weight[...]
     blocks, rows, lanes = sent.shape
     for i in range(blocks):
         sent[i] = total[:, i * lanes : (i + 1) * lanes].astype(jnp.bfloat16)
@@ -269,12 +289,13 @@
 
 
 def call(kernel, out_shape, flops, limit, *operands, scratch=()):
-    moved = sum(x.size * x.dtype.itemsize for x in operands) + out_shape.size * 2
+    arrays = (*operands, *jax.tree.leaves(out_shape))
+    moved = sum(x.size * x.dtype.itemsize for x in arrays)
     return pl.pallas_call(
         kernel,
         out_shape=out_shape,
         in_specs=[pl.BlockSpec(memory_space=pltpu.VMEM)] * len(operands),
-        out_specs=pl.BlockSpec(memory_space=pltpu.VMEM),
+        out_specs=jax.tree.map(lambda _: pl.BlockSpec(memory_space=pltpu.VMEM), out_shape),
         scratch_shapes=scratch,
         compiler_params=pltpu.CompilerParams(vmem_limit_bytes=limit << 20),
         cost_estimate=pl.CostEstimate(flops=flops, bytes_accessed=moved, transcendentals=0),
@@ -296,6 +317,12 @@
 
     own_wave = lax.dynamic_index_in_dim(assignment, slot, 0, keepdims=False)
     own_mask = lax.dynamic_index_in_dim(pattern, own_wave, 0, keepdims=False).astype(jnp.bfloat16)
+    lat_tiles, deg_tiles = own_mask.shape
+    wide_mask = jnp.broadcast_to(
+        own_mask[:, None, :, None], (lat_tiles, TILE, deg_tiles, TILE)
+    ).reshape(lat_count, degrees)
+    pruned = legendre[0] * wide_mask
+
     at_lats = forward(spectral[0], legendre[0], pattern, assignment)
     at_lats = at_lats.reshape(peers, lats, 2, channels)
     received = exchange(at_lats)
@@ -310,29 +337,18 @@
     split = jnp.roll(split, (-middle("y"), -middle("y")), (0, 3))
     mine = lax.dynamic_index_in_dim(split, core, 1, keepdims=False)
     wide = y_count * channels
-    spread = (
-        jnp.arange(wide, dtype=jnp.int32)[:, None] // F
-        == jnp.arange(wide // F, dtype=jnp.int32)[None, :]
-    ).astype(jnp.bfloat16)
-    same_field = (
-        jnp.arange(wide, dtype=jnp.int32)[:, None] % F
-        == jnp.arange(wide, dtype=jnp.int32)[None, :] % F
-    )
 
     def matrix(source):
         small = lax.dynamic_index_in_dim(mine, source, 3, keepdims=False)
-        small = small.reshape(wide // F, wide // F)
-        tall = jnp.einsum("pb,ab->pa", spread, small).astype(jnp.bfloat16)
-        full = jnp.einsum("pa,qa->pq", tall, spread).astype(jnp.bfloat16)
-        return jnp.where(same_field, full, jnp.zeros((), jnp.bfloat16))
+        return small.reshape(wide // F, wide // F)
 
     group = own_position()
     weight = lax.dynamic_slice_in_dim(quad_weight, group * lats, lats)
-    weight = jnp.broadcast_to(weight[None, :, None], (wave_total, lats, 2)).reshape(rows, 1)
-    own_matrix, other_matrix = matrix(core), matrix(1 - core)
-    received, synthesis, analysis, own_matrix, other_matrix, weight, own_mask = (
+    weight = jnp.broadcast_to(weight[:, None], (lats, wide))
+    own_small, other_small = matrix(core), matrix(1 - core)
+    received, synthesis, analysis, own_small, other_small, weight, pruned_t = (
         lax.optimization_barrier(
-            (received, synthesis, analysis, own_matrix, other_matrix, weight, own_mask)
+            (received, synthesis, analysis, own_small, other_small, weight, pruned.T)
         )
     )
 
@@ -346,18 +362,23 @@
         received,
         synthesis,
         analysis,
+        weight,
         scratch=[pltpu.VMEM((y_count, rows, channels), jnp.float32)] * 3
         + [pltpu.VMEM((lats, lon_count, wide), jnp.bfloat16)],
     )
     swapped = lax.ppermute(returned, "core", [(0, 1), (1, 0)])
 
-    begun = call(
+    begun, other_matrix = call(
         own_kernel,
-        jax.ShapeDtypeStruct((rows, wide), jnp.float32),
+        (
+            jax.ShapeDtypeStruct((rows, wide), jnp.float32),
+            jax.ShapeDtypeStruct((wide, wide), jnp.bfloat16),
+        ),
         2 * rows * wide * wide,
         16,
         returned,
-        own_matrix,
+        own_small,
+        other_small,
     )
     sent = call(
         couple_kernel,
@@ -367,14 +388,7 @@
         begun,
         swapped,
         other_matrix,
-        weight,
-    )
-    sent, own_mask = lax.optimization_barrier((sent, own_mask))
-    lat_tiles, deg_tiles = own_mask.shape
-    wide_mask = jnp.broadcast_to(
-        own_mask[:, None, :, None], (lat_tiles, TILE, deg_tiles, TILE)
-    ).reshape(lat_count, degrees)
-    pruned_t = (legendre[0] * wide_mask).T
+    )
     sent = sent.reshape(peers, lats, 2, channels)
     weighted = exchange(sent)
     tendency = backward(weighted.reshape(2 * lat_count, channels), pruned_t)

time: 117 us -> 116 us (level)
  blocking collectives: 0 us -> 48.9 us
  waiting for transfers between devices: 44.5 us -> 17.3 us
  starting transfers between devices: 48.3 us -> 28.8 us
  local copies, waits for them, and re-layouts: 9.94 us -> 8.27 us
    all_to_all x0 -> x1, blocking collectives: none -> 48.9 us  [exchange(): lax.all_to_all(values, tuple(SIZES), split_axis=0, concat_axis=0, axis_in...]
    all_to_all x2 -> x1, waiting for transfers between devices: 43.2 us -> 16.3 us  [exchange(): lax.all_to_all(values, tuple(SIZES), split_axis=0, concat_axis=0, axis_in...]
    all_to_all x2 -> x1, starting transfers between devices: 46.4 us -> 26.9 us  [exchange(): lax.all_to_all(values, tuple(SIZES), split_axis=0, concat_axis=0, axis_in...]
    unnamed x10 -> x12, local copies, waits for them, and re-layouts: 4.1 us -> 2.74 us
  transfers between devices with their start and end apart: 3 -> 2, of which waited for: 3 -> 2; matrix products, arithmetic and copies ran while one was open for 12% -> 9% of each run, Pallas kernels for 0% -> 1%
where the time goes in v9:
time: 116 us
  blocking collectives  48.9 us (42%)
  starting transfers between devices  28.8 us (25%)
  waiting for transfers between devices  17.3 us (15%)
  local copies, waits for them, and re-layouts  8.27 us (7%)
  Pallas kernels  7.47 us (6%)
  other arithmetic  2.74 us (2%)
  between operations  2.32 us (2%)
    all_to_all x1, blocking collectives, exchange(): lax.all_to_all(values, tuple(SIZES), split_axis=0, concat_axis=0, axis_in...  48.9 us
    all_to_all x1, starting transfers between devices, exchange(): lax.all_to_all(values, tuple(SIZES), split_axis=0, concat_axis=0, axis_in...  26.9 us
    all_to_all x1, waiting for transfers between devices, exchange(): lax.all_to_all(values, tuple(SIZES), split_axis=0, concat_axis=0, axis_in...  16.3 us
    pallas_call x1, Pallas kernels, forward(): pl.pallas_call(forward_kernel, out_shape=jax.ShapeDtypeStruct((2 * lat_co...  3.13 us
    pallas_call x3, Pallas kernels, call(): pl.pallas_call(kernel, out_shape=out_shape, in_specs=[pl.BlockSpec(memory...  2.86 us
    unnamed x12, local copies, waits for them, and re-layouts  2.74 us
  transfers between devices with their start and end apart: 2, of which 2 were waited for; matrix products, arithmetic and copies ran while one was open for 9% of the time, Pallas kernels for 1%

profile of v9, /device:TPU:6, one launch (start us, length us, event | category | flops | bytes accessed | tf_op | source)
XLA Modules:
  0.0 115.8 jit_solution(12171348065955107797)
XLA Ops:
  0.0 3.1 %shard_map.64 = bf16[2560,128]{1,0:T(8,128)(2,1)} custom-call(bf16[1280,128]{1,0:T(8,128)(2,1)} %bitcast.37, bf16[1280,640]{1,0:T(8,128)(2,1)} %bitcast.34, s32[10,5,64]{2,1,0:T(8,128)} %bitcast.38, s32[64]{0:T(128)} %assignment.1), custom_call_target="tpu_custom_call" | custom-call | tf_op jit(solution)/shard_map/pallas_call | solution.py:145
  3.1 26.9 %all-to-all-start = ((bf16[256,5,2,128]{3,2,1,0:T(2,128)(2,1)}), bf16[256,5,2,128]{3,2,1,0:T(2,128)(2,1)S(1)}, u32[]{:S(2)}, u32[]{:S(2)}) async-start(bf16[256,5,2,128]{3,2,1,0:T(2,128)(2,1)} %bitcast.36), calls=%async_computation | async-start | bytes 1310720 | tf_op jit(solution)/shard_map/all_to_all | solution.py:48
  30.0 0.6 dynamic_slice.23
  31.9 2.2 %copy.23 = bf16[1,1280,640]{1,2,0:T(8,128)(2,1)} copy(bf16[1,1280,640]{2,1,0:T(8,128)(2,1)S(1)} %copy-done) | data formatting | bytes 3276800 | tf_op args[1]
  34.9 0.1 copy.34
  35.1 0.4 broadcast_in_dim.5
  35.5 0.4 copy.39
  35.9 2.2 %copy.31 = bf16[1280,640]{0,1:T(8,128)(2,1)} copy(bf16[1280,640]{1,0:T(8,128)(2,1)S(1)} %bitcast.35) | data formatting | bytes 3276800 | tf_op jit(solution)/shard_map/reshape | solution.py:323
  38.1 0.1 slice.67
  38.3 0.1 slice.69
  38.5 0.2 fusion.10
  38.7 0.2 fusion.2
  39.7 0.8 dynamic_slice.22
  40.5 0.3 fusion.8
  40.9 2.1 %fusion.pruned_t = bf16[640,1280]{1,0:T(8,128)(2,1)S(1)} fusion(bf16[1280,640]{0,1:T(8,128)(2,1)} %copy.31, bf16[1,1280,640]{1,2,0:T(8,128)(2,1)} %copy.23), kind=kLoop, calls=%fused_computation.2 | loop fusion | flops 819200 | bytes 4915200 | tf_op jit(solution)/shard_map/transpose | solution.py:351
  43.0 16.3 %all-to-all-done = bf16[256,5,2,128]{3,2,1,0:T(2,128)(2,1)S(1)} async-done(((bf16[256,5,2,128]{3,2,1,0:T(2,128)(2,1)}), bf16[256,5,2,128]{3,2,1,0:T(2,128)(2,1)S(1)}, u32[]{:S(2)}, u32[]{:S(2)}) %all-to-all-start) | async-done | bytes 655392 | tf_op jit(solution)/shard_map/all_to_all | solution.py:48
  59.3 0.1 copy.32.synthesis
  59.5 1.3 %shard_map.65.own = bf16[640,512]{1,0:T(8,128)(2,1)S(1)} custom-call(bf16[4,640,128]{2,1,0:T(8,128)(2,1)S(1)} %bitcast.31, bf16[192,128]{1,0:T(8,128)(2,1)S(1)} %copy.32.synthesis, bf16[128,192]{1,0:T(8,128)(2,1)S(1)} %get-tuple-element.16.analysis, f32[5,512]{1,0:T(8,128)S(1)} %broadcast_in_dim.4.weight), custom_call_target="tpu_custom_call" | custom-call | flops 251658240 | bytes 1419264 | tf_op jit(solution)/shard_map/pallas_call | solution.py:294
  60.7 1.9 %collective-permute-start = (bf16[640,512]{1,0:T(8,128)(2,1)S(1)}, bf16[640,512]{1,0:T(8,128)(2,1)S(1)}, u32[]{:S(2)}, u32[]{:S(2)}) collective-permute-start(bf16[640,512]{1,0:T(8,128)(2,1)S(1)} %shard_map.65.own), channel_id=1, source_target_pairs={{0,1},{1,0},{2,3},{3,2},{4,5},{5,4},{6,7},{7,6},{8,9},{9,8},{10,11... | collective-permute-start | bytes 1966088 | tf_op jit(solution)/shard_map/ppermute | solution.py:369
  62.6 1.1 shard_map.66
  63.8 1.0 collective-permute-done.other
  64.7 0.5 shard_map.67
  65.2 48.9 %all_to_all.10 = bf16[256,5,2,128]{3,2,1,0:T(2,128)(2,1)S(1)} all-to-all(bf16[256,5,2,128]{3,2,1,0:T(2,128)(2,1)S(1)} %bitcast.32), channel_id=1, replica_groups={{276,308,340,372,404,436,468,500,20,52,84,116,148,180,212,244,284,316,3..., dimensions={0} | all-to-all | bytes 1310720 | tf_op jit(solution)/shard_map/all_to_all | solution.py:48
  114.1 1.5 %shard_map.68 = bf16[1280,128]{1,0:T(8,128)(2,1)} custom-call(bf16[2560,128]{1,0:T(8,128)(2,1)S(1)} %bitcast.30, bf16[640,1280]{1,0:T(8,128)(2,1)S(1)} %fusion.pruned_t), custom_call_target="tpu_custom_call" | custom-call | tf_op jit(solution)/shard_map/pallas_call | solution.py:275
  (27 shorter events, 1.2 us)
Async XLA Ops:
  0.0 30.0 %copy-start.3 = (s32[64]{0:T(128)S(1)}, s32[64]{0:T(128)}, u32[]{:S(2)}) copy-start(s32[64]{0:T(128)} %assignment.1) | copy-start | bytes 772
  0.0 31.9 %copy-start = (bf16[1,1280,640]{2,1,0:T(8,128)(2,1)S(1)}, bf16[1,1280,640]{2,1,0:T(8,128)(2,1)}, u32[]{:S(2)}) copy-start(bf16[1,1280,640]{2,1,0:T(8,128)(2,1)} %param.7) | copy-start | bytes 4915204
  3.1 56.1 %all-to-all-start = ((bf16[256,5,2,128]{3,2,1,0:T(2,128)(2,1)}), bf16[256,5,2,128]{3,2,1,0:T(2,128)(2,1)S(1)}, u32[]{:S(2)}, u32[]{:S(2)}) async-start(bf16[256,5,2,128]{3,2,1,0:T(2,128)(2,1)} %bitcast.36), calls=%async_computation | async-start | bytes 1310720 | tf_op jit(solution)/shard_map/all_to_all | solution.py:48
  31.9 2.9 %copy-start.1 = (s32[64,10,5]{0,2,1:T(8,128)S(1)}, s32[64,10,5]{0,2,1:T(8,128)}, u32[]{:S(2)}) copy-start(s32[64,10,5]{0,2,1:T(8,128)} %param.8) | copy-start | bytes 38404
  35.9 2.2 %copy-start.2 = (bf16[128,128]{1,0:T(8,128)(2,1)S(1)}, bf16[128,128]{1,0:T(8,128)(2,1)}, u32[]{:S(2)}) copy-start(bf16[128,128]{1,0:T(8,128)(2,1)} %param.11) | copy-start | bytes 98308
  60.7 4.0 %collective-permute-start = (bf16[640,512]{1,0:T(8,128)(2,1)S(1)}, bf16[640,512]{1,0:T(8,128)(2,1)S(1)}, u32[]{:S(2)}, u32[]{:S(2)}) collective-permute-start(bf16[640,512]{1,0:T(8,128)(2,1)S(1)} %shard_map.65.own), channel_id=1, source_target_pairs={{0,1},{1,0},{2,3},{3,2},{4,5},{5,4},{6,7},{7,6},{8,9},{9,8},{10,11... | collective-permute-start | bytes 1966088 | tf_op jit(solution)/shard_map/ppermute | solution.py:369

commit v10 on v9

--- a/solution.py
+++ b/solution.py
@@ -87,8 +87,10 @@
         span = pl.ds(i * chunk, chunk)
         return pltpu.make_async_copy(legendre.at[span], matrix.at[span], lat_sem.at[i])
 
+    depth = chunk // LAT_PARTS
+
     def out_copy(i):
-        span = pl.ds(2 * i * chunk, 2 * chunk)
+        span = pl.ds(2 * i * depth, 2 * depth)
         return pltpu.make_async_copy(merged.at[span], at_lats.at[span], out_sem.at[i])
 
     for i in range(LAT_CHUNKS):
@@ -117,7 +119,6 @@
             )
             tile = slice(TILE * t, TILE * (t + 1))
             matrix[tile, :] = matrix[tile, :] * keep
-        depth = chunk // LAT_PARTS
         founds = [
             jnp.dot(
                 matrix[pl.ds(chunk * i + depth * j, depth), :],
@@ -131,9 +132,12 @@
                 wide[pl.ds(2 * depth * j + part, depth, stride=2), :] = found[
                     :, part * lanes : (part + 1) * lanes
                 ]
-        merged[2 * chunk * i : 2 * chunk * (i + 1), :] = wide[...].astype(jnp.bfloat16)
-        out_copy(i).start()
-    for i in range(LAT_CHUNKS):
+            first = 2 * (chunk * i + depth * j)
+            merged[first : first + 2 * depth, :] = wide[
+                2 * depth * j : 2 * depth * (j + 1), :
+            ].astype(jnp.bfloat16)
+            out_copy(i * LAT_PARTS + j).start()
+    for i in range(LAT_CHUNKS * LAT_PARTS):
         out_copy(i).wait()
 
 
@@ -158,7 +162,7 @@
             pltpu.VMEM((2 * lat_count, channels), jnp.bfloat16),
             pltpu.SemaphoreType.DMA((3,)),
             pltpu.SemaphoreType.DMA((LAT_CHUNKS,)),
-            pltpu.SemaphoreType.DMA((LAT_CHUNKS,)),
+            pltpu.SemaphoreType.DMA((LAT_CHUNKS * LAT_PARTS,)),
         ],
     )(spectral.reshape(2 * degrees, channels), legendre, pattern, assignment)
 

time: 116 us -> 116 us (level)
  no operation moved by 1% of the time
where the time goes in v10:
time: 116 us
  blocking collectives  48.9 us (42%)
  starting transfers between devices  28.8 us (25%)
  waiting for transfers between devices  17.3 us (15%)
  local copies, waits for them, and re-layouts  8.27 us (7%)
  Pallas kernels  7.49 us (6%)
  other arithmetic  2.74 us (2%)
  between operations  2.32 us (2%)
    all_to_all x1, blocking collectives, exchange(): lax.all_to_all(values, tuple(SIZES), split_axis=0, concat_axis=0, axis_in...  48.9 us
    all_to_all x1, starting transfers between devices, exchange(): lax.all_to_all(values, tuple(SIZES), split_axis=0, concat_axis=0, axis_in...  26.9 us
    all_to_all x1, waiting for transfers between devices, exchange(): lax.all_to_all(values, tuple(SIZES), split_axis=0, concat_axis=0, axis_in...  16.3 us
    pallas_call x1, Pallas kernels, forward(): pl.pallas_call(forward_kernel, out_shape=jax.ShapeDtypeStruct((2 * lat_co...  3.15 us
    pallas_call x3, Pallas kernels, call(): pl.pallas_call(kernel, out_shape=out_shape, in_specs=[pl.BlockSpec(memory...  2.86 us
    unnamed x12, local copies, waits for them, and re-layouts  2.74 us
  transfers between devices with their start and end apart: 2, of which 2 were waited for; matrix products, arithmetic and copies ran while one was open for 9% of the time, Pallas kernels for 1%

profile of v10, /device:TPU:6, one launch (start us, length us, event | category | flops | bytes accessed | tf_op | source)
XLA Modules:
  0.0 115.8 jit_solution(13534031776998538010)
XLA Ops:
  0.0 3.2 %shard_map.64 = bf16[2560,128]{1,0:T(8,128)(2,1)} custom-call(bf16[1280,128]{1,0:T(8,128)(2,1)} %bitcast.37, bf16[1280,640]{1,0:T(8,128)(2,1)} %bitcast.34, s32[10,5,64]{2,1,0:T(8,128)} %bitcast.38, s32[64]{0:T(128)} %assignment.1), custom_call_target="tpu_custom_call" | custom-call | tf_op jit(solution)/shard_map/pallas_call | solution.py:149
  3.2 26.9 %all-to-all-start = ((bf16[256,5,2,128]{3,2,1,0:T(2,128)(2,1)}), bf16[256,5,2,128]{3,2,1,0:T(2,128)(2,1)S(1)}, u32[]{:S(2)}, u32[]{:S(2)}) async-start(bf16[256,5,2,128]{3,2,1,0:T(2,128)(2,1)} %bitcast.36), calls=%async_computation | async-start | bytes 1310720 | tf_op jit(solution)/shard_map/all_to_all | solution.py:48
  30.1 0.6 dynamic_slice.23
  32.0 2.2 %copy.23 = bf16[1,1280,640]{1,2,0:T(8,128)(2,1)} copy(bf16[1,1280,640]{2,1,0:T(8,128)(2,1)S(1)} %copy-done) | data formatting | bytes 3276800 | tf_op args[1]
  34.9 0.1 copy.34
  35.1 0.4 broadcast_in_dim.5
  35.6 0.4 copy.39
  36.0 2.2 %copy.31 = bf16[1280,640]{0,1:T(8,128)(2,1)} copy(bf16[1280,640]{1,0:T(8,128)(2,1)S(1)} %bitcast.35) | data formatting | bytes 3276800 | tf_op jit(solution)/shard_map/reshape | solution.py:327
  38.2 0.1 slice.67
  38.3 0.1 slice.69
  38.5 0.2 fusion.10
  38.7 0.2 fusion.2
  39.7 0.8 dynamic_slice.22
  40.5 0.3 fusion.8
  40.9 2.1 %fusion.pruned_t = bf16[640,1280]{1,0:T(8,128)(2,1)S(1)} fusion(bf16[1280,640]{0,1:T(8,128)(2,1)} %copy.31, bf16[1,1280,640]{1,2,0:T(8,128)(2,1)} %copy.23), kind=kLoop, calls=%fused_computation.2 | loop fusion | flops 819200 | bytes 4915200 | tf_op jit(solution)/shard_map/transpose | solution.py:355
  43.0 16.3 %all-to-all-done = bf16[256,5,2,128]{3,2,1,0:T(2,128)(2,1)S(1)} async-done(((bf16[256,5,2,128]{3,2,1,0:T(2,128)(2,1)}), bf16[256,5,2,128]{3,2,1,0:T(2,128)(2,1)S(1)}, u32[]{:S(2)}, u32[]{:S(2)}) %all-to-all-start) | async-done | bytes 655392 | tf_op jit(solution)/shard_map/all_to_all | solution.py:48
  59.4 0.1 copy.32.synthesis
  59.5 1.3 %shard_map.65.own = bf16[640,512]{1,0:T(8,128)(2,1)S(1)} custom-call(bf16[4,640,128]{2,1,0:T(8,128)(2,1)S(1)} %bitcast.31, bf16[192,128]{1,0:T(8,128)(2,1)S(1)} %copy.32.synthesis, bf16[128,192]{1,0:T(8,128)(2,1)S(1)} %get-tuple-element.16.analysis, f32[5,512]{1,0:T(8,128)S(1)} %broadcast_in_dim.4.weight), custom_call_target="tpu_custom_call" | custom-call | flops 251658240 | bytes 1419264 | tf_op jit(solution)/shard_map/pallas_call | solution.py:298
  60.7 1.9 %collective-permute-start = (bf16[640,512]{1,0:T(8,128)(2,1)S(1)}, bf16[640,512]{1,0:T(8,128)(2,1)S(1)}, u32[]{:S(2)}, u32[]{:S(2)}) collective-permute-start(bf16[640,512]{1,0:T(8,128)(2,1)S(1)} %shard_map.65.own), channel_id=1, source_target_pairs={{0,1},{1,0},{2,3},{3,2},{4,5},{5,4},{6,7},{7,6},{8,9},{9,8},{10,11... | collective-permute-start | bytes 1966088 | tf_op jit(solution)/shard_map/ppermute | solution.py:373
  62.7 1.1 shard_map.66
  63.8 1.0 collective-permute-done.other
  64.7 0.5 shard_map.67
  65.2 48.9 %all_to_all.10 = bf16[256,5,2,128]{3,2,1,0:T(2,128)(2,1)S(1)} all-to-all(bf16[256,5,2,128]{3,2,1,0:T(2,128)(2,1)S(1)} %bitcast.32), channel_id=1, replica_groups={{276,308,340,372,404,436,468,500,20,52,84,116,148,180,212,244,284,316,3..., dimensions={0} | all-to-all | bytes 1310720 | tf_op jit(solution)/shard_map/all_to_all | solution.py:48
  114.1 1.5 %shard_map.68 = bf16[1280,128]{1,0:T(8,128)(2,1)} custom-call(bf16[2560,128]{1,0:T(8,128)(2,1)S(1)} %bitcast.30, bf16[640,1280]{1,0:T(8,128)(2,1)S(1)} %fusion.pruned_t), custom_call_target="tpu_custom_call" | custom-call | tf_op jit(solution)/shard_map/pallas_call | solution.py:279
  (27 shorter events, 1.2 us)
Async XLA Ops:
  0.0 30.1 %copy-start.3 = (s32[64]{0:T(128)S(1)}, s32[64]{0:T(128)}, u32[]{:S(2)}) copy-start(s32[64]{0:T(128)} %assignment.1) | copy-start | bytes 772
  0.0 31.9 %copy-start = (bf16[1,1280,640]{2,1,0:T(8,128)(2,1)S(1)}, bf16[1,1280,640]{2,1,0:T(8,128)(2,1)}, u32[]{:S(2)}) copy-start(bf16[1,1280,640]{2,1,0:T(8,128)(2,1)} %param.7) | copy-start | bytes 4915204
  3.2 56.1 %all-to-all-start = ((bf16[256,5,2,128]{3,2,1,0:T(2,128)(2,1)}), bf16[256,5,2,128]{3,2,1,0:T(2,128)(2,1)S(1)}, u32[]{:S(2)}, u32[]{:S(2)}) async-start(bf16[256,5,2,128]{3,2,1,0:T(2,128)(2,1)} %bitcast.36), calls=%async_computation | async-start | bytes 1310720 | tf_op jit(solution)/shard_map/all_to_all | solution.py:48
  32.0 2.9 %copy-start.1 = (s32[64,10,5]{0,2,1:T(8,128)S(1)}, s32[64,10,5]{0,2,1:T(8,128)}, u32[]{:S(2)}) copy-start(s32[64,10,5]{0,2,1:T(8,128)} %param.8) | copy-start | bytes 38404
  35.9 2.2 %copy-start.2 = (bf16[128,128]{1,0:T(8,128)(2,1)S(1)}, bf16[128,128]{1,0:T(8,128)(2,1)}, u32[]{:S(2)}) copy-start(bf16[128,128]{1,0:T(8,128)(2,1)} %param.11) | copy-start | bytes 98308
  60.7 4.0 %collective-permute-start = (bf16[640,512]{1,0:T(8,128)(2,1)S(1)}, bf16[640,512]{1,0:T(8,128)(2,1)S(1)}, u32[]{:S(2)}, u32[]{:S(2)}) collective-permute-start(bf16[640,512]{1,0:T(8,128)(2,1)S(1)} %shard_map.65.own), channel_id=1, source_target_pairs={{0,1},{1,0},{2,3},{3,2},{4,5},{5,4},{6,7},{7,6},{8,9},{9,8},{10,11... | collective-permute-start | bytes 1966088 | tf_op jit(solution)/shard_map/ppermute | solution.py:373
